TPU v7x, 32 devices: a whole 2x2x4 slice. The times are simulated.
32 devices in a mesh: groups: 2 (over y), wide: 4 (over z), narrow: 2 (over x), inner: 2 (over core).
Axes of the slice: x: 2, y: 2, z: 4, core: 2. Of those that a mesh axis runs over, the one named last changes fastest.
Arguments:
- tokens: bfloat16 [128, 6144], P(('groups', 'wide'), ('narrow', 'inner')), parts along dimension 0, may hold values from -6 to 6
- cotangent: bfloat16 [128, 6144], P(('groups', 'wide'), ('narrow', 'inner')), parts along dimension 0, may hold values from -3 to 3
- w_gate: bfloat16 [6144, 16384], P(('narrow', 'inner'), 'wide'), may hold values from -0.078125 to 0.078125
- w_up: bfloat16 [6144, 16384], P(('narrow', 'inner'), 'wide'), may hold values from -0.078125 to 0.078125
- w_down: bfloat16 [16384, 6144], P('wide', ('narrow', 'inner')), may hold values from -0.046875 to 0.046875
Outputs:
- output: bfloat16 [128, 6144], P(('groups', 'wide'), ('narrow', 'inner')), parts along dimension 0
- grad_input: bfloat16 [128, 6144], P(('groups', 'wide'), ('narrow', 'inner')), parts along dimension 0
- grad_wgate: bfloat16 [12288, 16384], P(('groups', 'narrow', 'inner'), 'wide'), parts along dimension 0
- grad_wup: bfloat16 [12288, 16384], P(('groups', 'narrow', 'inner'), 'wide'), parts along dimension 0
- grad_wdown: bfloat16 [32768, 6144], P(('groups', 'wide'), ('narrow', 'inner')), parts along dimension 0
There are 2 independent parts, one for each index of `groups`. A program takes and returns all parts, laid end to end along the dimension named above; an argument that names none is the same for every part. Nothing has to cross between parts.
All inputs are finite; a program needn't handle non-finite values.
Results may differ from a plain program's by a relative error of at most 0.012.
Values may be sent and summed in bfloat16 or wider, within the bound.
No kernel may reach another device: no remote copies, remote signals or barrier semaphores. Data moves between devices by JAX's collectives and lax.ppermute only.
A program may use at most 192 MiB of HBM per device.

v0:
```python
import jax
import jax.numpy as jnp
from jax import lax
from jax.sharding import PartitionSpec as P


def contract_last(left, right):
    return lax.dot_general(
        left, right, (((1,), (1,)), ((), ())), preferred_element_type=jnp.float32
    )


def contract_first(left, right):
    return lax.dot_general(
        left, right, (((0,), (0,)), ((), ())), preferred_element_type=jnp.float32
    )


def activate(gate, up):
    return (gate * jax.nn.sigmoid(gate) * up).astype(jnp.bfloat16)


def grad_parts(gate, up, upstream):
    sigmoid_gate = jax.nn.sigmoid(gate)
    grad_gate = (upstream * up * sigmoid_gate * (1.0 + gate * (1.0 - sigmoid_gate))).astype(
        jnp.bfloat16
    )
    grad_up = (upstream * gate * sigmoid_gate).astype(jnp.bfloat16)
    return (grad_gate, grad_up)


def body(tokens, cotangent, w_gate, w_up, w_down):
    gathered = lax.all_gather(tokens, "wide", axis=0, tiled=True)
    gate_part = jnp.dot(gathered, w_gate, preferred_element_type=jnp.float32)
    up_part = jnp.dot(gathered, w_up, preferred_element_type=jnp.float32)
    gate, up = lax.psum((gate_part, up_part), ("narrow", "inner"))
    hidden = activate(gate, up)
    output = lax.psum_scatter(
        jnp.dot(hidden, w_down, preferred_element_type=jnp.float32).astype(jnp.bfloat16),
        "wide",
        scatter_dimension=0,
        tiled=True,
    )
    cot_all = lax.all_gather(cotangent, "wide", axis=0, tiled=True)
    upstream_part = contract_last(cot_all, w_down)
    grad_wdown = contract_first(hidden, cot_all).astype(jnp.bfloat16)
    upstream = lax.psum(upstream_part, ("narrow", "inner"))
    grad_gate, grad_up = grad_parts(gate, up, upstream)
    grad_input = lax.psum_scatter(
        (contract_last(grad_gate, w_gate) + contract_last(grad_up, w_up)).astype(jnp.bfloat16),
        "wide",
        scatter_dimension=0,
        tiled=True,
    )
    grad_wgate = contract_first(gathered, grad_gate).astype(jnp.bfloat16)
    grad_wup = contract_first(gathered, grad_up).astype(jnp.bfloat16)
    return (output, grad_input, grad_wgate, grad_wup, grad_wdown)


def solution(mesh):
    return jax.shard_map(
        body,
        mesh=mesh,
        in_specs=(
            P(("groups", "wide"), ("narrow", "inner")),
            P(("groups", "wide"), ("narrow", "inner")),
            P(("narrow", "inner"), "wide"),
            P(("narrow", "inner"), "wide"),
            P("wide", ("narrow", "inner")),
        ),
        out_specs=(
            P(("groups", "wide"), ("narrow", "inner")),
            P(("groups", "wide"), ("narrow", "inner")),
            P(("groups", "narrow", "inner"), "wide"),
            P(("groups", "narrow", "inner"), "wide"),
            P(("groups", "wide"), ("narrow", "inner")),
        ),
        check_vma=False,
    )
```

profile of v0, /device:TPU:0, one launch (start us, length us, event | category | flops | bytes accessed | tf_op | source)
XLA Modules:
  0.0 206.2 jit_solution(17270711638761119251)
XLA Ops:
  7.2 0.0 all-reduce.3.cloned.1.call-start
  7.2 0.0 copy-start
  7.2 15.8 %all_gather.6 = bf16[64,1536]{1,0:T(8,128)(2,1)S(1)} all-gather(bf16[16,1536]{1,0:T(8,128)(2,1)} %param.5), channel_id=1, replica_groups=mesh['groups'=2,'wide'=4,'narrow'=2,'inner'=2] {'wide'}, dimensions={0}, use_global_device_ids=true | all-gather | bytes 245760 | tf_op jit(solution)/shard_map/all_gather | solution.py:33
  23.0 0.0 slice-start
  23.0 0.0 slice-start.1
  23.0 8.0 %fusion.4 = f32[64,4096]{1,0:T(8,128)} fusion(bf16[64,1536]{1,0:T(8,128)(2,1)S(1)} %all_gather.6, bf16[1536,4096]{1,0:T(8,128)(2,1)} %param.8), kind=kOutput, calls=%fused_computation.13 | convolution fusion | flops 805306368 | bytes 13828096 | tf_op jit(solution)/shard_map/dot_general | solution.py:35
  31.0 0.0 copy-done
  31.0 0.0 copy-start.1
  31.0 0.0 slice-start.2
  31.0 3.3 %fusion.3 = f32[64,4096]{1,0:T(8,128)} fusion(bf16[64,1536]{1,0:T(8,128)(2,1)S(1)} %all_gather.6, bf16[1536,4096]{1,0:T(8,128)(2,1)S(1)} %copy-done), kind=kOutput, calls=%fused_computation.12 | convolution fusion | flops 805306368 | bytes 13828096 | tf_op jit(solution)/shard_map/dot_general | solution.py:34
  34.3 0.0 copy-done.1
  34.3 14.0 %all_gather.7 = bf16[64,1536]{1,0:T(8,128)(2,1)S(1)} all-gather(bf16[16,1536]{1,0:T(8,128)(2,1)S(1)} %copy-done.1), channel_id=1, replica_groups=mesh['groups'=2,'wide'=4,'narrow'=2,'inner'=2] {'wide'}, dimensions={0}, use_global_device_ids=true | all-gather | bytes 245760 | tf_op jit(solution)/shard_map/all_gather | solution.py:44
  48.3 0.0 slice-done
  48.3 0.0 slice-done.1
  48.3 0.0 slice-done.2
  48.3 4.9 %fusion.5 = f32[64,4096]{1,0:T(8,128)} fusion(bf16[64,1536]{1,0:T(8,128)(2,1)S(1)} %all_gather.7, bf16[4096,1536]{1,0:T(8,128)(2,1)S(1)} %bitcast.23), kind=kOutput, calls=%fused_computation.14 | convolution fusion | flops 805306368 | bytes 13828096 | tf_op jit(solution)/shard_map/dot_general | solution.py:8
  53.2 0.0 all-reduce.3.cloned.1.call-update
  53.2 0.0 reduce-scatter.3.cloned.1.call-start
  53.3 69.9 %all-reduce.3.cloned.1.call-done = (f32[64,4096]{1,0:T(8,128)}, f32[64,4096]{1,0:T(8,128)}, f32[64,4096]{1,0:T(8,128)}) async-done(((f32[64,4096]{1,0:T(8,128)}, f32[64,4096]{1,0:T(8,128)}, f32[64,4096]{1,0:T(8,128)}), (f32[64,4096]{1,0:T(8,128)}, f32[64,4096]{1,0:T(8,128)}, f32[64,4096]{1,0:T(8,128)})) %all-reduce.3.cloned.1.call-update) | async-done | bytes 3145744 | tf_op jit(solution)/shard_map/psum | solution.py:36
  123.2 2.4 %multiply_convert_fusion = (bf16[64,4096]{1,0:T(8,128)(2,1)S(1)}, bf16[64,4096]{1,0:T(8,128)(2,1)S(1)}, bf16[64,4096]{1,0:T(8,128)(2,1)S(1)}) fusion(f32[64,4096]{1,0:T(8,128)} %get-tuple-element.12, f32[64,4096]{1,0:T(8,128)} %get-tuple-element.11, f32[64,4096]{1,0:T(8,128)} %get-tuple-element.10), kind=kLoop, calls=%fused_computation.8 | loop fusion | flops 4194304 | bytes 4718592 | tf_op jit(solution)/shard_map/convert_element_type | solution.py:28
  125.6 0.0 slice-start.3
  125.6 0.0 slice-start.4
  125.6 8.7 %fusion.6 = f32[64,1536]{1,0:T(8,128)S(1)} fusion(bf16[64,4096]{1,0:T(8,128)(2,1)S(1)} %get-tuple-element.14, bf16[1536,4096]{1,0:T(8,128)(2,1)} %param.7), kind=kOutput, calls=%fused_computation.15 | convolution fusion | flops 805306368 | bytes 13500416 | tf_op jit(solution)/shard_map/dot_general | solution.py:8
  134.3 0.0 slice-start.5
  134.3 6.6 %fusion = bf16[1536,4096]{0,1:T(8,128)(2,1)} fusion(bf16[64,4096]{1,0:T(8,128)(2,1)S(1)} %get-tuple-element.14, bf16[64,1536]{1,0:T(8,128)(2,1)S(1)} %all_gather.6), kind=kOutput, calls=%fused_computation.3 | convolution fusion | flops 811597824 | bytes 13303808 | tf_op jit(solution)/shard_map/dot_general | solution.py:14
  140.9 0.0 slice-done.3
  140.9 0.0 slice-done.4
  140.9 0.0 slice-done.5
  141.0 3.0 %convolution_convert_fusion.3 = bf16[64,1536]{1,0:T(8,128)(2,1)} fusion(bf16[64,4096]{1,0:T(8,128)(2,1)S(1)} %get-tuple-element.15, bf16[4096,1536]{1,0:T(8,128)(2,1)S(1)} %bitcast.25), kind=kOutput, calls=%fused_computation.7 | convolution fusion | flops 805404672 | bytes 13303808 | tf_op jit(solution)/shard_map/dot_general | solution.py:39
  143.9 0.0 reduce-scatter.3.cloned.1.call-update
  144.0 0.2 reduce-scatter.5.cloned.1.call-start
  144.2 6.4 %fusion.1 = bf16[1536,4096]{0,1:T(8,128)(2,1)} fusion(bf16[64,4096]{1,0:T(8,128)(2,1)S(1)} %get-tuple-element.13, bf16[64,1536]{1,0:T(8,128)(2,1)S(1)} %all_gather.6), kind=kOutput, calls=%fused_computation.4 | convolution fusion | flops 811597824 | bytes 13303808 | tf_op jit(solution)/shard_map/dot_general | solution.py:14
  150.6 9.2 %fusion.2 = bf16[64,1536]{1,0:T(8,128)(2,1)} fusion(f32[64,1536]{1,0:T(8,128)S(1)} %fusion.6, bf16[64,4096]{1,0:T(8,128)(2,1)S(1)} %get-tuple-element.13, bf16[1536,4096]{1,0:T(8,128)(2,1)} %param.8), kind=kOutput, calls=%fused_computation.6 | convolution fusion | flops 805502976 | bytes 13697024 | tf_op jit(solution)/shard_map/dot_general | solution.py:8
  159.8 0.0 reduce-scatter.5.cloned.1.call-update
  159.8 6.6 %convolution_convert_fusion = bf16[4096,1536]{1,0:T(8,128)(2,1)} fusion(bf16[64,4096]{1,0:T(8,128)(2,1)S(1)} %get-tuple-element.15, bf16[64,1536]{1,0:T(8,128)(2,1)S(1)} %all_gather.7), kind=kOutput, calls=%fused_computation | convolution fusion | flops 811597824 | bytes 13303808 | tf_op jit(solution)/shard_map/dot_general | solution.py:14
  166.4 16.6 %copy.10 = bf16[1536,4096]{1,0:T(8,128)(2,1)} copy(bf16[1536,4096]{0,1:T(8,128)(2,1)} %fusion) | data formatting | bytes 25165824
  183.0 16.6 %copy.11 = bf16[1536,4096]{1,0:T(8,128)(2,1)} copy(bf16[1536,4096]{0,1:T(8,128)(2,1)} %fusion.1) | data formatting | bytes 25165824
  199.6 0.0 reduce-scatter.3.cloned.1.call-done
  199.6 0.0 reduce-scatter.5.cloned.1.call-done
  (2 shorter events, 0.0 us)
Async XLA Ops:
  7.2 116.0 %all-reduce.3.cloned.1.call-start = ((), (), s32[]{:S(2)}) async-start(), calls=%async_computation.4 | async-start | bytes 6291456 | tf_op jit(solution)/shard_map/psum | solution.py:36
  7.2 23.8 %copy-start = (bf16[1536,4096]{1,0:T(8,128)(2,1)S(1)}, bf16[1536,4096]{1,0:T(8,128)(2,1)}, u32[]{:S(2)}) copy-start(bf16[1536,4096]{1,0:T(8,128)(2,1)} %param.7) | copy-start | bytes 37748740
  23.0 25.3 %slice-start = ((s8[12582912]{0:T(1024)(128)(4,1)}), s8[4194304]{0:T(1024)(128)(4,1)S(1)}, s32[]{:S(2)}) async-start(s8[12582912]{0:T(1024)(128)(4,1)} %bitcast.22), calls=%async_computation.5 | async-start | bytes 8388608
  23.0 25.3 %slice-start.1 = ((s8[12582912]{0:T(1024)(128)(4,1)}), s8[4194304]{0:T(1024)(128)(4,1)S(1)}, s32[]{:S(2)}) async-start(s8[12582912]{0:T(1024)(128)(4,1)} %bitcast.22), calls=%async_computation.6 | async-start | bytes 8388608
  31.0 3.3 %copy-start.1 = (bf16[16,1536]{1,0:T(8,128)(2,1)S(1)}, bf16[16,1536]{1,0:T(8,128)(2,1)}, u32[]{:S(2)}) copy-start(bf16[16,1536]{1,0:T(8,128)(2,1)} %param.6) | copy-start | bytes 147460
  31.0 17.3 %slice-start.2 = ((s8[12582912]{0:T(1024)(128)(4,1)}), s8[4194304]{0:T(1024)(128)(4,1)S(1)}, s32[]{:S(2)}) async-start(s8[12582912]{0:T(1024)(128)(4,1)} %bitcast.22), calls=%async_computation.7 | async-start | bytes 8388608
  53.2 146.4 %reduce-scatter.3.cloned.1.call-start = ((), (), s32[]{:S(2)}) async-start(), calls=%async_computation.2 | async-start | bytes 245760 | tf_op jit(solution)/shard_map/reduce_scatter | solution.py:38
  125.6 15.3 %slice-start.3 = ((s8[12582912]{0:T(1024)(128)(4,1)}), s8[4194304]{0:T(1024)(128)(4,1)S(1)}, s32[]{:S(2)}) async-start(s8[12582912]{0:T(1024)(128)(4,1)} %bitcast.24), calls=%async_computation.8 | async-start | bytes 8388608
  125.6 15.3 %slice-start.4 = ((s8[12582912]{0:T(1024)(128)(4,1)}), s8[4194304]{0:T(1024)(128)(4,1)S(1)}, s32[]{:S(2)}) async-start(s8[12582912]{0:T(1024)(128)(4,1)} %bitcast.24), calls=%async_computation.9 | async-start | bytes 8388608
  134.3 6.6 %slice-start.5 = ((s8[12582912]{0:T(1024)(128)(4,1)}), s8[4194304]{0:T(1024)(128)(4,1)S(1)}, s32[]{:S(2)}) async-start(s8[12582912]{0:T(1024)(128)(4,1)} %bitcast.24), calls=%async_computation.10 | async-start | bytes 8388608
  144.0 55.7 %reduce-scatter.5.cloned.1.call-start = ((), (), s32[]{:S(2)}) async-start(), calls=%async_computation.3 | async-start | bytes 245760 | tf_op jit(solution)/shard_map/reduce_scatter | solution.py:49
Sparse Core Ops, SparseCore 0:
  53.3 69.8 all-reduce.2
  144.1 19.4 reduce-scatter.2
  166.5 17.5 reduce-scatter.4
where the time goes:
time: 207 us; the launch traced here: 206 us
  waiting for transfers between devices  70 us (34%)
  matrix products  56.6 us (27%)
  local copies, waits for them, and re-layouts  33.3 us (16%)
  blocking collectives  29.8 us (14%)
  between operations  13.8 us (7%)
  other arithmetic  2.4 us (1%)
    psum x1, waiting for transfers between devices, body(): gate, up = lax.psum((gate_part, up_part), ('narrow', 'inner'))  69.9 us
    unnamed x18, local copies, waits for them, and re-layouts  33.3 us
    dot_general x3, matrix products, contract_last(): lax.dot_general(left, right, (((1,), (1,)), ((), ())), preferred_element_...  22.7 us
    dot_general x3, matrix products, contract_first(): lax.dot_general(left, right, (((0,), (0,)), ((), ())), preferred_element_...  19.7 us
    all_gather x1, blocking collectives, body(): gathered = lax.all_gather(tokens, 'wide', axis=0, tiled=True)  15.8 us
    all_gather x1, blocking collectives, body(): cot_all = lax.all_gather(cotangent, 'wide', axis=0, tiled=True)  14 us
    dot_general x1, matrix products, body(): up_part = jnp.dot(gathered, w_up, preferred_element_type=jnp.float32)  7.99 us
  transfers between devices with their start and end apart: 3, of which 1 were waited for; matrix products, arithmetic and copies ran while one was open for 27% of the time, Pallas kernels for 0%

commit v1 on v0

v1 whole, which is shorter than its diff:
```python
import functools

import jax
import jax.numpy as jnp
from jax import lax
from jax.experimental import pallas as pl
from jax.experimental.pallas import tpu as pltpu
from jax.sharding import PartitionSpec as P

F32 = jnp.float32
BF16 = jnp.bfloat16
CHUNKS = 2
VMEM_SPEC = pl.BlockSpec(memory_space=pltpu.VMEM)
SMEM_SPEC = pl.BlockSpec(memory_space=pltpu.SMEM)
HBM_SPEC = pl.BlockSpec(memory_space=pltpu.MemorySpace.HBM)
LIMIT = 6 << 20
SCALE = 100


def contract(left, right, left_dim, right_dim):
    return lax.dot_general(
        left, right, (((left_dim,), (right_dim,)), ((), ())), preferred_element_type=F32
    )


def params(**more):
    return pltpu.CompilerParams(vmem_limit_bytes=LIMIT, **more)


def cost(flops, moved):
    return pl.CostEstimate(
        flops=int(flops) // SCALE, bytes_accessed=int(moved) // SCALE, transcendentals=0
    )


def shift(x, axis, size, by):
    return lax.ppermute(x, axis, [(i, (i + by) % size) for i in range(size)])


def column(me_ref, part, inner, width):
    chunk, core = part
    return pl.multiple_of((chunk * inner + lax.rem(me_ref[0] + core, inner)) * width, 128)


def in_vmem(shape, dtype):
    return pltpu.VMEM(shape, dtype)


def in_hbm(x):
    return pltpu.with_memory_space_constraint(x, pltpu.MemorySpace.HBM)


def part_copies(start, whole, part, sems):
    here = pl.ds(start, part[2].shape[0])
    return [
        pltpu.make_async_copy(whole[0].at[:, here], part[0], sems.at[0]),
        pltpu.make_async_copy(whole[1].at[:, here], part[1], sems.at[1]),
        pltpu.make_async_copy(whole[2].at[here, :], part[2], sems.at[2]),
    ]


def part_shapes(weights, width):
    features = weights[0].shape[0]
    return [
        in_vmem((features, width), BF16),
        in_vmem((features, width), BF16),
        in_vmem((width, features), BF16),
    ]


def load_kernel(parts, inner, *refs):
    me, whole, out, sems = refs[0], refs[1:4], refs[4:-1], refs[-1]
    copies = []
    for i, part in enumerate(parts):
        dest = out[3 * i : 3 * i + 3]
        start = column(me, part, inner, dest[2].shape[0])
        copies += part_copies(start, whole, dest, sems.at[i])
    for copy in copies:
        copy.start()
    for copy in copies:
        copy.wait()


def load(me, parts, inner, weights, width):
    outs = part_shapes(weights, width) * len(parts)
    out = pl.pallas_call(
        functools.partial(load_kernel, parts, inner),
        in_specs=[SMEM_SPEC] + [HBM_SPEC] * 3,
        out_specs=[VMEM_SPEC] * len(outs),
        out_shape=outs,
        scratch_shapes=[pltpu.SemaphoreType.DMA((len(parts), 3))],
        compiler_params=params(),
        cost_estimate=cost(0, 6 * len(parts) * width * weights[0].shape[0]),
        name="load_weights",
    )(me, *weights)
    return [tuple(out[3 * i : 3 * i + 3]) for i in range(len(parts))]


def pack_kernel(tokens, cot, packed):
    rows = tokens.shape[0]
    packed[:rows, :] = tokens[...]
    packed[rows:, :] = cot[...]


def pack(tokens, cot):
    return pl.pallas_call(
        pack_kernel,
        in_specs=[VMEM_SPEC] * 2,
        out_specs=VMEM_SPEC,
        out_shape=in_vmem((2 * tokens.shape[0], tokens.shape[1]), BF16),
        compiler_params=params(),
        name="pack_rows",
    )(tokens, cot)


def forward_kernel(rows, tile, pieces, loads, inner, out_dtype, *refs):
    refs = list(refs)
    take = lambda n: [refs.pop(0) for _ in range(n)]
    me = take(1)[0] if loads else None
    acts, weights = take(pieces or 2), take(3)
    whole = take(3) if loads else None
    sums = take(1)[0]
    if pieces:
        tokens_ref, cot_ref = take(2)
    else:
        tokens_ref, cot_ref = acts
    copies = []
    if loads:
        part = take(3)
        start = column(me, loads, inner, part[2].shape[0])
        copies = part_copies(start, whole, part, take(1)[0])
    for copy in copies:
        copy.start()
    if pieces:
        for k, piece in enumerate(acts):
            tokens_ref[pl.ds(k * rows, rows), :] = piece[:rows, :]
            cot_ref[pl.ds(k * rows, rows), :] = piece[rows:, :]

    def columns(step):
        here = pl.ds(pl.multiple_of(step * tile, 128), tile)
        tokens, cot = tokens_ref[...], cot_ref[...]
        sums[0, :, here] = contract(tokens, weights[0][:, here], 1, 0).astype(out_dtype)
        sums[1, :, here] = contract(tokens, weights[1][:, here], 1, 0).astype(out_dtype)
        sums[2, :, here] = contract(cot, weights[2][here, :], 1, 1).astype(out_dtype)

    steps = sums.shape[2] // tile
    if loads:
        pl.loop(0, steps)(columns)
    else:
        for step in range(steps):
            columns(step)
    for copy in copies:
        copy.wait()


def forward(me, inner, acts, part, rows, out_dtype, loads=(), whole=()):
    pieces = len(acts) if len(acts) != 2 else 0
    whole = whole if loads else ()
    width, features = part[2].shape
    total = rows * pieces if pieces else acts[0].shape[0]
    outs = [in_vmem((3, total, width), out_dtype)]
    if pieces:
        outs += [in_vmem((total, features), BF16)] * 2
    if loads:
        outs += part_shapes(whole, width)
    return pl.pallas_call(
        functools.partial(
            forward_kernel, rows, min(256, width), pieces, loads, inner, out_dtype
        ),
        in_specs=[SMEM_SPEC] * bool(loads)
        + [VMEM_SPEC] * (len(acts) + 3)
        + [HBM_SPEC] * len(whole),
        out_specs=[VMEM_SPEC] * len(outs),
        out_shape=outs,
        scratch_shapes=[pltpu.SemaphoreType.DMA((3,))] * bool(loads),
        compiler_params=params(),
        cost_estimate=cost(6 * total * width * features, 6 * width * features),
        name="partial_sums",
    )(*([me] * bool(loads)), *acts, *part, *whole)


def join_kernel(mine, received, kept, sent):
    total = mine[...] + received[...].astype(F32)
    kept[...] = total
    sent[...] = total.astype(BF16)


def join(mine, received):
    return pl.pallas_call(
        join_kernel,
        in_specs=[VMEM_SPEC] * 2,
        out_specs=[VMEM_SPEC] * 2,
        out_shape=[in_vmem(mine.shape, F32), in_vmem(mine.shape, BF16)],
        compiler_params=params(),
        cost_estimate=cost(mine.size, 12 * mine.size),
        name="join_cores",
    )(mine, received)


def activate_kernel(*refs):
    kept, received, out = refs[0], refs[1:-1], refs[-1]
    gate, up, upstream = [
        sum((r[i].astype(F32) for r in received), kept[i]) for i in range(3)
    ]
    sigmoid = 1.0 / (1.0 + jnp.exp(-gate))
    swish = gate * sigmoid
    out[0] = (swish * up).astype(BF16)
    out[1] = (upstream * up * sigmoid * (1.0 + gate * (1.0 - sigmoid))).astype(BF16)
    out[2] = (upstream * swish).astype(BF16)


def activate(kept, received):
    return pl.pallas_call(
        activate_kernel,
        in_specs=[VMEM_SPEC] * (1 + len(received)),
        out_specs=VMEM_SPEC,
        out_shape=in_vmem(kept.shape, BF16),
        compiler_params=params(),
        cost_estimate=cost(8 * kept.size, 8 * kept.size),
        name="activation",
    )(kept, *received)


def backward_kernel(where, inner, tile, rows, grads, first, fresh, last, *refs):
    refs = list(refs)
    take = lambda n: [refs.pop(0) for _ in range(n)]
    parts = len(where)
    me = take(1)[0]
    acts = take(parts)
    weights = [take(3) for _ in range(parts)] if rows else None
    tokens, cot = take(2) if grads else (None, None)
    before = take(2) if rows and not first else None
    if grads and not fresh:
        take(3)
    sums = take(1 + last if last else 2) if rows else None
    outs = take(3) if grads else None
    out_acc, grad_acc = (take(2) if last else sums) if rows else (None, None)
    if grads:
        wide, tall, sems = take(3)
    width = acts[0].shape[2]
    steps = width // tile

    def copies(slot, at):
        here = pl.ds(pl.multiple_of(at, 128), tile)
        return [
            pltpu.make_async_copy(wide.at[slot, 0], outs[0].at[:, here], sems.at[slot, 0]),
            pltpu.make_async_copy(wide.at[slot, 1], outs[1].at[:, here], sems.at[slot, 1]),
            pltpu.make_async_copy(tall.at[slot], outs[2].at[here, :], sems.at[slot, 2]),
        ]

    if rows:
        if first:
            out_acc[...] = jnp.zeros_like(out_acc)
            grad_acc[...] = jnp.zeros_like(grad_acc)
        else:
            out_acc[...] = before[0][...]
            grad_acc[...] = before[1][...]
    count = 0
    for p in range(parts):
        for j in range(steps):
            here = slice(j * tile, (j + 1) * tile)
            hidden, grad_gate, grad_up = [acts[p][i, :, here] for i in range(3)]
            if grads:
                slot = count % 2
                at = column(me, where[p], inner, width) + j * tile
                if count >= 2:
                    for copy in copies(slot, at):
                        copy.wait()
                wide[slot, 0] = contract(tokens[...], grad_gate, 0, 0).astype(BF16)
                wide[slot, 1] = contract(tokens[...], grad_up, 0, 0).astype(BF16)
                tall[slot] = contract(hidden, cot[...], 0, 0).astype(BF16)
                for copy in copies(slot, at):
                    copy.start()
            if rows:
                w_gate, w_up, w_down = weights[p]
                out_acc[...] += contract(hidden, w_down[here, :], 1, 0)
                grad_acc[...] += contract(grad_gate, w_gate[:, here], 1, 1) + contract(
                    grad_up, w_up[:, here], 1, 1
                )
            count += 1
    if last:
        n = sums[0].shape[0] // 2
        for k, ref in enumerate(sums):
            ref[:n, :] = out_acc[k * n : (k + 1) * n, :].astype(ref.dtype)
            ref[n:, :] = grad_acc[k * n : (k + 1) * n, :].astype(ref.dtype)
    if grads:
        for back in range(min(2, count)):
            for copy in copies((count - 1 - back) % 2, 0):
                copy.wait()


def backward(me, where, inner, acts, weights, tokens, cot, before, grads, hidden, last_rows=0):
    parts = len(acts)
    total, width = acts[0].shape[1:]
    features = tokens.shape[1]
    rows, makes = before is not None, grads is not None
    tile = min(256, width)
    args, specs, outs, out_specs, scratch = [me, *acts], [], [], [], []
    if rows:
        args += [w for part in weights for w in part]
    if makes:
        args += [tokens, cot]
    if rows:
        args += before
    specs = [SMEM_SPEC] + [VMEM_SPEC] * (len(args) - 1)
    aliases = {}
    if rows:
        if last_rows:
            shape = (2 * last_rows, features)
            outs += [in_vmem(shape, F32)] + [in_vmem(shape, BF16)] * (total // last_rows - 1)
            scratch += [pltpu.VMEM((total, features), F32)] * 2
        else:
            outs += [in_vmem((total, features), F32)] * 2
        out_specs += [VMEM_SPEC] * len(outs)
    if makes:
        aliases = {len(args) + i: len(outs) + i for i in range(len(grads))}
        args += grads
        specs += [HBM_SPEC] * len(grads)
        outs += [
            pltpu.HBM((features, hidden), BF16),
            pltpu.HBM((features, hidden), BF16),
            pltpu.HBM((hidden, features), BF16),
        ]
        out_specs += [HBM_SPEC] * 3
        scratch += [
            pltpu.VMEM((2, 2, features, tile), BF16),
            pltpu.VMEM((2, tile, features), BF16),
            pltpu.SemaphoreType.DMA((2, 3)),
        ]
    work = 6 * total * width * features * parts
    out = pl.pallas_call(
        functools.partial(
            backward_kernel, where, inner, tile, rows, makes, not before, not grads,
            total // last_rows - 1 if last_rows else 0,
        ),
        in_specs=specs,
        out_specs=out_specs,
        out_shape=outs,
        scratch_shapes=scratch,
        input_output_aliases=aliases,
        compiler_params=params(),
        cost_estimate=cost(work * (rows + makes), 6 * width * features * parts * (rows + makes)),
        name="output_rows" if not makes else "weight_grads" if not rows else "backward",
    )(*args)
    return (out[:-3], out[-3:]) if makes else (out, None)


def finish_kernel(*refs):
    mine, received, (output, grad_input) = refs[0], refs[1:-2], refs[-2:]
    rows = output.shape[0]
    total = mine[...]
    for r in received:
        total = total + r[...].astype(F32)
    output[...] = total[:rows].astype(BF16)
    grad_input[...] = total[rows:].astype(BF16)


def finish(mine, received):
    shape = jax.ShapeDtypeStruct((mine.shape[0] // 2, mine.shape[1]), BF16)
    return pl.pallas_call(
        finish_kernel,
        in_specs=[VMEM_SPEC] * (1 + len(received)),
        out_specs=[VMEM_SPEC] * 2,
        out_shape=[shape] * 2,
        compiler_params=params(),
        name="finish_rows",
    )(mine, *received)


def body(sizes, tokens, cotangent, w_gate, w_up, w_down):
    wide, narrow, inner = sizes["wide"], sizes["narrow"], sizes["inner"]
    rows = tokens.shape[0]
    hidden = w_gate.shape[1]
    weights = tuple(in_hbm(w) for w in (w_gate, w_up, w_down))
    width = hidden // (CHUNKS * inner)
    me = lax.axis_index("inner").astype(jnp.int32).reshape(1)
    order = [(c, core) for c in range(CHUNKS) for core in (1, 0)]

    packed = pack(tokens, cotangent)
    acts = [packed] + [shift(packed, "wide", wide, k) for k in range(1, wide)]
    parts = load(me, order[:2], inner, weights, width)
    acts, parts = lax.optimization_barrier((acts, parts))
    kept, sent, crossed = [], [], []
    for chunk in range(CHUNKS):
        at = 2 * chunk
        made = []
        for i, dtype in ((at, BF16), (at + 1, F32)):
            ahead = order[i + 2] if i + 2 < len(order) else ()
            out = forward(me, inner, acts, parts[i], rows, dtype, ahead, weights)
            made.append(out[0])
            if len(acts) != 2:
                acts = out[1:3]
            if ahead:
                parts.append(tuple(out[-3:]))
        total, out = join(made[1], shift(made[0], "inner", inner, 1))
        kept.append(total)
        sent.append(out)
        acts, _ = lax.optimization_barrier((acts, out))
        crossed.append([shift(out, "narrow", narrow, k) for k in range(1, narrow)])
    tokens_all, cot_all = acts
    crossed[0], _ = lax.optimization_barrier((crossed[0], sent))
    sums, grads, later = (), (), None
    for chunk in range(CHUNKS):
        at = 2 * chunk
        own = activate(kept[chunk], crossed[chunk])
        other = shift(own, "inner", inner, 1)
        both = [(order[at + 1], own, parts[at + 1]), (order[at], other, parts[at])]
        if chunk < CHUNKS - 1:
            where, what, which = zip(*both)
            sums, grads = backward(
                me, where, inner, what, which, tokens_all, cot_all, sums, grads, hidden
            )
            crossed[chunk + 1], sums = lax.optimization_barrier((crossed[chunk + 1], sums))
        else:
            for i, (where, what, which) in enumerate(both):
                sums, _ = backward(
                    me, [where], inner, [what], [which], tokens_all, cot_all, sums, None,
                    hidden, rows if i else 0,
                )
            where, what, _ = zip(*both)
    back = [shift(sums[k], "wide", wide, -k) for k in range(1, wide)]
    _, grads = backward(
        me, where, inner, what, None, tokens_all, cot_all, None, grads, hidden
    )
    output, grad_input = finish(sums[0], back)
    return (output, grad_input, *grads)


def solution(mesh):
    rows = P(("groups", "wide"), ("narrow", "inner"))
    return jax.shard_map(
        functools.partial(body, dict(mesh.shape)),
        mesh=mesh,
        in_specs=(
            rows,
            rows,
            P(("narrow", "inner"), "wide"),
            P(("narrow", "inner"), "wide"),
            P("wide", ("narrow", "inner")),
        ),
        out_specs=(
            rows,
            rows,
            P(("groups", "narrow", "inner"), "wide"),
            P(("groups", "narrow", "inner"), "wide"),
            P(("groups", "wide"), ("narrow", "inner")),
        ),
        check_vma=False,
    )
```

time: 207 us -> 70.6 us (0.34)
  waiting for transfers between devices: 70 us -> 8.59 us
  matrix products: 56.6 us -> 0 us
  Pallas kernels: 0 us -> 44.9 us
  local copies, waits for them, and re-layouts: 33.3 us -> 1.59 us
  blocking collectives: 29.8 us -> 0 us
  starting transfers between devices: 0.3 us -> 14.4 us
  between operations: 13.8 us -> 0.81 us
  other arithmetic: 2.4 us -> 0 us
    psum x1 -> x0, waiting for transfers between devices: 69.9 us -> none  [body(): gate, up = lax.psum((gate_part, up_part), ('narrow', 'inner'))]
    dot_general x9 -> x0, matrix products: 56.6 us -> none  [the longest x3 22.7 us: contract_last(): lax.dot_general(left, right, (((1,), (1,)), ((), ())), preferred_element_...]
    pallas_call x0 -> x15, Pallas kernels: none -> 44.9 us  [the longest x4 25.1 us: backward(): pl.pallas_call(functools.partial(backward_kernel, where, inner, tile, row...]
    unnamed x18 -> x4, local copies, waits for them, and re-layouts: 33.3 us -> 1.59 us
    all_gather x2 -> x0, blocking collectives: 29.8 us -> none  [the longest x1 15.8 us: body(): gathered = lax.all_gather(tokens, 'wide', axis=0, tiled=True)]
    ppermute x0 -> x12, starting transfers between devices: none -> 14.4 us  [shift(): return lax.ppermute(x, axis, [(i, (i + by) % size) for i in range(size)])]
    ppermute x0 -> x12, waiting for transfers between devices: none -> 8.59 us  [shift(): return lax.ppermute(x, axis, [(i, (i + by) % size) for i in range(size)])]
    convert_element_type x1 -> x0, other arithmetic: 2.4 us -> none  [grad_parts(): grad_up = (upstream * gate * sigmoid_gate).astype(jnp.bfloat16)]
  transfers between devices with their start and end apart: 3 -> 12, of which waited for: 1 -> 3; matrix products, arithmetic and copies ran while one was open for 27% -> 0% of each run, Pallas kernels for 0% -> 50%
where the time goes in v1:
time: 70.6 us; the launch traced here: 70.3 us
  Pallas kernels  44.9 us (64%)
  starting transfers between devices  14.4 us (20%)
  waiting for transfers between devices  8.59 us (12%)
  local copies, waits for them, and re-layouts  1.59 us (2%)
  between operations  0.81 us (1%)
    pallas_call x4, Pallas kernels, backward(): pl.pallas_call(functools.partial(backward_kernel, where, inner, tile, row...  25.1 us
    ppermute x12, starting transfers between devices, shift(): return lax.ppermute(x, axis, [(i, (i + by) % size) for i in range(size)])  14.4 us
    pallas_call x4, Pallas kernels, forward(): pl.pallas_call(functools.partial(forward_kernel, rows, min(256, width), p...  12 us
    ppermute x12, waiting for transfers between devices, shift(): return lax.ppermute(x, axis, [(i, (i + by) % size) for i in range(size)])  8.59 us
    pallas_call x1, Pallas kernels, load(): pl.pallas_call(functools.partial(load_kernel, parts, inner), in_specs=[SM...  6.54 us
    unnamed x4, local copies, waits for them, and re-layouts  1.59 us
  transfers between devices with their start and end apart: 12, of which 3 were waited for; matrix products, arithmetic and copies ran while one was open for 0% of the time, Pallas kernels for 50%

profile of v1, /device:TPU:0, one launch (start us, length us, event | category | flops | bytes accessed | tf_op | source)
XLA Modules:
  0.0 70.3 jit_solution(798071353529540220)
XLA Ops:
  0.6 0.0 copy-start
  0.6 0.8 %copy-done = bf16[16,1536]{1,0:T(8,128)(2,1)S(1)} copy-done((bf16[16,1536]{1,0:T(8,128)(2,1)S(1)}, bf16[16,1536]{1,0:T(8,128)(2,1)}, u32[]{:S(2)}) %copy-start) | copy-done | bytes 49176
  1.4 0.0 copy-start.1
  1.4 0.8 %copy-done.1 = bf16[16,1536]{1,0:T(8,128)(2,1)S(1)} copy-done((bf16[16,1536]{1,0:T(8,128)(2,1)S(1)}, bf16[16,1536]{1,0:T(8,128)(2,1)}, u32[]{:S(2)}) %copy-start.1) | copy-done | bytes 49176
  2.2 5.1 %collective-permute-start.2 = (bf16[32,1536]{1,0:T(8,128)(2,1)S(1)}, bf16[32,1536]{1,0:T(8,128)(2,1)S(1)}, u32[]{:S(2)}, u32[]{:S(2)}) collective-permute-start(bf16[32,1536]{1,0:T(8,128)(2,1)S(1)} %pack_rows.1.refs_1_), channel_id=1, source_target_pairs={{0,12},{4,0},{8,4},{12,8},{1,13},{5,1},{9,5},{13,9},{2,14},{6,2},{... | collective-permute-start | bytes 294920 | tf_op jit(solution)/shard_map/ppermute | solution.py:37
  7.3 0.0 collective-permute-start.1
  7.3 1.0 %collective-permute-start = (bf16[32,1536]{1,0:T(8,128)(2,1)S(1)}, bf16[32,1536]{1,0:T(8,128)(2,1)S(1)}, u32[]{:S(2)}, u32[]{:S(2)}) collective-permute-start(bf16[32,1536]{1,0:T(8,128)(2,1)S(1)} %pack_rows.1.refs_1_), channel_id=1, source_target_pairs={{0,4},{4,8},{8,12},{12,0},{1,5},{5,9},{9,13},{13,1},{2,6},{6,10},{... | collective-permute-start | bytes 294920 | tf_op jit(solution)/shard_map/ppermute | solution.py:37
  8.3 6.5 %load_weights.1 = (bf16[1536,1024]{1,0:T(8,128)(2,1)S(1)}, bf16[1536,1024]{1,0:T(8,128)(2,1)S(1)}, bf16[1024,1536]{1,0:T(8,128)(2,1)S(1)}, bf16[1536,1024]{1,0:T...) custom-call(s32[1]{0:T(128)} %bitcast.refs_0_, bf16[1536,4096]{1,0:T(8,128)(2,1)} %refs_6_.1, ...), custom_call_target="tpu_custom_call" | custom-call | bytes 188743 | tf_op jit(solution)/shard_map/load_weights/pallas_call | solution.py:86
  14.9 0.0 collective-permute-done.2.refs_4_
  14.9 1.2 %collective-permute-done.1.refs_3_ = bf16[32,1536]{1,0:T(8,128)(2,1)S(1)} collective-permute-done((bf16[32,1536]{1,0:T(8,128)(2,1)S(1)}, bf16[32,1536]{1,0:T(8,128)(2,1)S(1)}, u32[]{:S(2)}, u32[]{:S(2)}) %collective-permute-start.1) | collective-permute-done | bytes 98336 | tf_op jit(solution)/shard_map/ppermute | solution.py:37
  16.1 0.0 collective-permute-done.refs_2_
  16.1 3.8 %partial_sums.4 = (bf16[3,64,1024]{2,1,0:T(8,128)(2,1)S(1)}, bf16[64,1536]{1,0:T(8,128)(2,1)S(1)}, bf16[64,1536]{1,0:T(8,128)(2,1)S(1)}, bf16[1536,1024]{1,0:T(8...) custom-call(s32[1]{0:T(128)} %bitcast.refs_0_, bf16[32,1536]{1,0:T(8,128)(2,1)S(1)} %pack_rows.1.refs_1_, ...), custom_call_target="tpu_custom_call" | custom-call | flops 6039797 | bytes 94371 | tf_op jit(solution)/shard_map/partial_sums/pallas_call | solution.py:166
  19.9 0.1 collective-permute-start.3
  20.0 3.8 %partial_sums.5 = (f32[3,64,1024]{2,1,0:T(8,128)S(1)}, bf16[1536,1024]{1,0:T(8,128)(2,1)S(1)}, bf16[1536,1024]{1,0:T(8,128)(2,1)S(1)}, bf16[1024,1536]{1,0:T(8,128)(2,1)S(1)}) custom-call(s32[1]{0:T(128)} %bitcast.refs_0_, bf16[64,1536]{1,0:T(8,128)(2,1)S(1)} %get-tuple-element.92.refs_1_.refs_0_.refs_9_.refs_3_, ...), custom_call_target="tpu_custom_call" | custom-call | flops 6039797 | bytes 94371 | tf_op jit(solution)/shard_map/partial_sums/pallas_call | solution.py:166
  23.8 0.0 collective-permute-done.3.received
  23.8 0.1 join_cores.2
  23.9 2.2 %partial_sums.7 = bf16[3,64,1024]{2,1,0:T(8,128)(2,1)S(1)} custom-call(bf16[64,1536]{1,0:T(8,128)(2,1)S(1)} %get-tuple-element.92.refs_1_.refs_0_.refs_9_.refs_3_, bf16[64,1536]{1,0:T(8,128)(2,1)S(1)} %get-tuple-element.93.refs_2_.refs_1_.refs_10_.refs_4_, bf16[1536,1024]{1,0:T(8,128)(2,1)S(1)} %get-tuple-element.85.refs_2_, ...), custom_call_target="tpu_custom_call" | custom-call | flops 6039797 | bytes 94371 | tf_op jit(solution)/shard_map/partial_sums/pallas_call | solution.py:166
  26.1 0.6 collective-permute-start.4
  26.7 1.5 %collective-permute-start.6 = (bf16[3,64,1024]{2,1,0:T(8,128)(2,1)S(1)}, bf16[3,64,1024]{2,1,0:T(8,128)(2,1)S(1)}, u32[]{:S(2)}, u32[]{:S(2)}) collective-permute-start(bf16[3,64,1024]{2,1,0:T(8,128)(2,1)S(1)} %get-tuple-element.79), channel_id=1, source_target_pairs={{0,2},{2,0},{1,3},{3,1},{4,6},{6,4},{5,7},{7,5},{8,10},{10,8},{9,1... | collective-permute-start | bytes 1179656 | tf_op jit(solution)/shard_map/ppermute | solution.py:37
  28.2 2.2 %partial_sums.6.mine = f32[3,64,1024]{2,1,0:T(8,128)S(1)} custom-call(bf16[64,1536]{1,0:T(8,128)(2,1)S(1)} %get-tuple-element.92.refs_1_.refs_0_.refs_9_.refs_3_, bf16[64,1536]{1,0:T(8,128)(2,1)S(1)} %get-tuple-element.93.refs_2_.refs_1_.refs_10_.refs_4_, bf16[1536,1024]{1,0:T(8,128)(2,1)S(1)} %get-tuple-element.82.refs_2_, ...), custom_call_target="tpu_custom_call" | custom-call | flops 6039797 | bytes 94371 | tf_op jit(solution)/shard_map/partial_sums/pallas_call | solution.py:166
  30.4 0.0 collective-permute-done.4.received
  30.4 0.1 join_cores.3
  30.5 7.2 %collective-permute-done.6.refs_1_ = bf16[3,64,1024]{2,1,0:T(8,128)(2,1)S(1)} collective-permute-done((bf16[3,64,1024]{2,1,0:T(8,128)(2,1)S(1)}, bf16[3,64,1024]{2,1,0:T(8,128)(2,1)S(1)}, u32[]{:S(2)}, u32[]{:S(2)}) %collective-permute-start.6) | collective-permute-done | bytes 393248 | tf_op jit(solution)/shard_map/ppermute | solution.py:37
  37.8 0.2 activation.2.refs_1_
  38.0 0.1 collective-permute-start.7
  38.0 1.6 %collective-permute-start.5 = (bf16[3,64,1024]{2,1,0:T(8,128)(2,1)S(1)}, bf16[3,64,1024]{2,1,0:T(8,128)(2,1)S(1)}, u32[]{:S(2)}, u32[]{:S(2)}) collective-permute-start(bf16[3,64,1024]{2,1,0:T(8,128)(2,1)S(1)} %get-tuple-element.89), channel_id=1, source_target_pairs={{0,2},{2,0},{1,3},{3,1},{4,6},{6,4},{5,7},{7,5},{8,10},{10,8},{9,1... | collective-permute-start | bytes 1179656 | tf_op jit(solution)/shard_map/ppermute | solution.py:37
  39.6 0.1 collective-permute-done.7.refs_2_
  39.7 11.0 %backward.1 = (f32[64,1536]{1,0:T(8,128)S(1)}, f32[64,1536]{1,0:T(8,128)S(1)}, bf16[1536,4096]{1,0:T(8,128)(2,1)}, bf16[1536,4096]{1,0:T(8,128)(2,1)}, bf16[4096,1536]{1,0:T(8,128)(2,1)}) custom-call(s32[1]{0:T(128)} %bitcast.refs_0_, bf16[3,64,1024]{2,1,0:T(8,128)(2,1)S(1)} %activation.2.refs_1_, bf16[3,64,1024]{2,1,0:T(8,128)(2,1)S(1)} %collective-permute-done.7.refs_2_, ...), custom_call_target="tpu_custom_call" | custom-call | flops 24159192 | bytes 377487 | tf_op jit(solution)/shard_map/backward/pallas_call | solution.py:331
  50.7 0.0 collective-permute-done.5.refs_1_
  50.7 0.2 activation.3.refs_1_
  51.0 0.2 collective-permute-start.8
  51.2 2.7 %output_rows.2 = (f32[64,1536]{1,0:T(8,128)S(1)}, f32[64,1536]{1,0:T(8,128)S(1)}) custom-call(s32[1]{0:T(128)} %bitcast.refs_0_, bf16[3,64,1024]{2,1,0:T(8,128)(2,1)S(1)} %activation.3.refs_1_, bf16[1536,1024]{1,0:T(8,128)(2,1)S(1)} %get-tuple-element.82.refs_2_, bf16[1536,1024]{1,0:T(8,128)(2,1)S(1)} %get-tuple-element.83.refs_3_, ...), custom_call_target="tpu_custom_call" | custom-call | flops 6039797 | bytes 94371 | tf_op jit(solution)/shard_map/output_rows/pallas_call | solution.py:331
  53.9 0.0 collective-permute-done.8.refs_1_.refs_2_
  53.9 2.6 %output_rows.3 = (f32[32,1536]{1,0:T(8,128)S(1)}, bf16[32,1536]{1,0:T(8,128)(2,1)S(1)}, bf16[32,1536]{1,0:T(8,128)(2,1)S(1)}, bf16[32,1536]{1,0:T(8,128)(2,1)S(1)}) custom-call(s32[1]{0:T(128)} %bitcast.refs_0_, bf16[3,64,1024]{2,1,0:T(8,128)(2,1)S(1)} %collective-permute-done.8.refs_1_.refs_2_, bf16[1536,1024]{1,0:T(8,128)(2,1)S(1)} %get-tuple-element.85.refs_2_, ...), custom_call_target="tpu_custom_call" | custom-call | flops 6039797 | bytes 94371 | tf_op jit(solution)/shard_map/output_rows/pallas_call | solution.py:331
  56.5 2.0 %collective-permute-start.9 = (bf16[32,1536]{1,0:T(8,128)(2,1)S(1)}, bf16[32,1536]{1,0:T(8,128)(2,1)S(1)}, u32[]{:S(2)}, u32[]{:S(2)}) collective-permute-start(bf16[32,1536]{1,0:T(8,128)(2,1)S(1)} %get-tuple-element.102), channel_id=1, source_target_pairs={{0,12},{4,0},{8,4},{12,8},{1,13},{5,1},{9,5},{13,9},{2,14},{6,2},{... | collective-permute-start | bytes 294920 | tf_op jit(solution)/shard_map/ppermute | solution.py:37
  58.5 0.8 %collective-permute-start.10 = (bf16[32,1536]{1,0:T(8,128)(2,1)S(1)}, bf16[32,1536]{1,0:T(8,128)(2,1)S(1)}, u32[]{:S(2)}, u32[]{:S(2)}) collective-permute-start(bf16[32,1536]{1,0:T(8,128)(2,1)S(1)} %get-tuple-element.103), channel_id=1, source_target_pairs={{0,8},{4,12},{8,0},{12,4},{1,9},{5,13},{9,1},{13,5},{2,10},{6,14},... | collective-permute-start | bytes 294920 | tf_op jit(solution)/shard_map/ppermute | solution.py:37
  59.3 1.5 %collective-permute-start.11 = (bf16[32,1536]{1,0:T(8,128)(2,1)S(1)}, bf16[32,1536]{1,0:T(8,128)(2,1)S(1)}, u32[]{:S(2)}, u32[]{:S(2)}) collective-permute-start(bf16[32,1536]{1,0:T(8,128)(2,1)S(1)} %get-tuple-element.104), channel_id=1, source_target_pairs={{0,4},{4,8},{8,12},{12,0},{1,5},{5,9},{9,13},{13,1},{2,6},{6,10},{... | collective-permute-start | bytes 294920 | tf_op jit(solution)/shard_map/ppermute | solution.py:37
  60.8 8.8 %weight_grads.1 = (bf16[1536,4096]{1,0:T(8,128)(2,1)}, bf16[1536,4096]{1,0:T(8,128)(2,1)}, bf16[4096,1536]{1,0:T(8,128)(2,1)}) custom-call(s32[1]{0:T(128)} %bitcast.refs_0_, bf16[3,64,1024]{2,1,0:T(8,128)(2,1)S(1)} %activation.3.refs_1_, ...), custom_call_target="tpu_custom_call", output_to_operand_aliasing={{0}: (5, {}), {1}: (6, {}), {2}: (7, {})} | custom-call | flops 12079595 | bytes 188743 | tf_op jit(solution)/shard_map/weight_grads/pallas_call | solution.py:331
  69.6 0.0 collective-permute-done.9.refs_1_
  69.6 0.0 collective-permute-done.10.refs_2_
  69.7 0.0 collective-permute-done.11.refs_3_
  69.7 0.7 finish_rows.1
  (1 shorter events, 0.0 us)
Async XLA Ops:
  0.6 0.8 %copy-start = (bf16[16,1536]{1,0:T(8,128)(2,1)S(1)}, bf16[16,1536]{1,0:T(8,128)(2,1)}, u32[]{:S(2)}) copy-start(bf16[16,1536]{1,0:T(8,128)(2,1)} %tokens.1) | copy-start | bytes 147460
  1.4 0.8 %copy-start.1 = (bf16[16,1536]{1,0:T(8,128)(2,1)S(1)}, bf16[16,1536]{1,0:T(8,128)(2,1)}, u32[]{:S(2)}) copy-start(bf16[16,1536]{1,0:T(8,128)(2,1)} %cot.1) | copy-start | bytes 147460
  2.2 12.7 %collective-permute-start.2 = (bf16[32,1536]{1,0:T(8,128)(2,1)S(1)}, bf16[32,1536]{1,0:T(8,128)(2,1)S(1)}, u32[]{:S(2)}, u32[]{:S(2)}) collective-permute-start(bf16[32,1536]{1,0:T(8,128)(2,1)S(1)} %pack_rows.1.refs_1_), channel_id=1, source_target_pairs={{0,12},{4,0},{8,4},{12,8},{1,13},{5,1},{9,5},{13,9},{2,14},{6,2},{... | collective-permute-start | bytes 294920 | tf_op jit(solution)/shard_map/ppermute | solution.py:37
  7.3 8.7 %collective-permute-start.1 = (bf16[32,1536]{1,0:T(8,128)(2,1)S(1)}, bf16[32,1536]{1,0:T(8,128)(2,1)S(1)}, u32[]{:S(2)}, u32[]{:S(2)}) collective-permute-start(bf16[32,1536]{1,0:T(8,128)(2,1)S(1)} %pack_rows.1.refs_1_), channel_id=1, source_target_pairs={{0,8},{4,12},{8,0},{12,4},{1,9},{5,13},{9,1},{13,5},{2,10},{6,14},... | collective-permute-start | bytes 294920 | tf_op jit(solution)/shard_map/ppermute | solution.py:37
  7.3 8.7 %collective-permute-start = (bf16[32,1536]{1,0:T(8,128)(2,1)S(1)}, bf16[32,1536]{1,0:T(8,128)(2,1)S(1)}, u32[]{:S(2)}, u32[]{:S(2)}) collective-permute-start(bf16[32,1536]{1,0:T(8,128)(2,1)S(1)} %pack_rows.1.refs_1_), channel_id=1, source_target_pairs={{0,4},{4,8},{8,12},{12,0},{1,5},{5,9},{9,13},{13,1},{2,6},{6,10},{... | collective-permute-start | bytes 294920 | tf_op jit(solution)/shard_map/ppermute | solution.py:37
  19.9 3.9 %collective-permute-start.3 = (bf16[3,64,1024]{2,1,0:T(8,128)(2,1)S(1)}, bf16[3,64,1024]{2,1,0:T(8,128)(2,1)S(1)}, u32[]{:S(2)}, u32[]{:S(2)}) collective-permute-start(bf16[3,64,1024]{2,1,0:T(8,128)(2,1)S(1)} %get-tuple-element.78), channel_id=1, source_target_pairs={{0,1},{1,0},{2,3},{3,2},{4,5},{5,4},{6,7},{7,6},{8,9},{9,8},{10,11... | collective-permute-start | bytes 1179656 | tf_op jit(solution)/shard_map/ppermute | solution.py:37
  26.1 4.3 %collective-permute-start.4 = (bf16[3,64,1024]{2,1,0:T(8,128)(2,1)S(1)}, bf16[3,64,1024]{2,1,0:T(8,128)(2,1)S(1)}, u32[]{:S(2)}, u32[]{:S(2)}) collective-permute-start(bf16[3,64,1024]{2,1,0:T(8,128)(2,1)S(1)} %partial_sums.7), channel_id=1, source_target_pairs={{0,1},{1,0},{2,3},{3,2},{4,5},{5,4},{6,7},{7,6},{8,9},{9,8},{10,11... | collective-permute-start | bytes 1179656 | tf_op jit(solution)/shard_map/ppermute | solution.py:37
  26.7 11.1 %collective-permute-start.6 = (bf16[3,64,1024]{2,1,0:T(8,128)(2,1)S(1)}, bf16[3,64,1024]{2,1,0:T(8,128)(2,1)S(1)}, u32[]{:S(2)}, u32[]{:S(2)}) collective-permute-start(bf16[3,64,1024]{2,1,0:T(8,128)(2,1)S(1)} %get-tuple-element.79), channel_id=1, source_target_pairs={{0,2},{2,0},{1,3},{3,1},{4,6},{6,4},{5,7},{7,5},{8,10},{10,8},{9,1... | collective-permute-start | bytes 1179656 | tf_op jit(solution)/shard_map/ppermute | solution.py:37
  38.0 1.8 %collective-permute-start.7 = (bf16[3,64,1024]{2,1,0:T(8,128)(2,1)S(1)}, bf16[3,64,1024]{2,1,0:T(8,128)(2,1)S(1)}, u32[]{:S(2)}, u32[]{:S(2)}) collective-permute-start(bf16[3,64,1024]{2,1,0:T(8,128)(2,1)S(1)} %activation.2.refs_1_), channel_id=1, source_target_pairs={{0,1},{1,0},{2,3},{3,2},{4,5},{5,4},{6,7},{7,6},{8,9},{9,8},{10,11... | collective-permute-start | bytes 1179656 | tf_op jit(solution)/shard_map/ppermute | solution.py:37
  38.0 12.7 %collective-permute-start.5 = (bf16[3,64,1024]{2,1,0:T(8,128)(2,1)S(1)}, bf16[3,64,1024]{2,1,0:T(8,128)(2,1)S(1)}, u32[]{:S(2)}, u32[]{:S(2)}) collective-permute-start(bf16[3,64,1024]{2,1,0:T(8,128)(2,1)S(1)} %get-tuple-element.89), channel_id=1, source_target_pairs={{0,2},{2,0},{1,3},{3,1},{4,6},{6,4},{5,7},{7,5},{8,10},{10,8},{9,1... | collective-permute-start | bytes 1179656 | tf_op jit(solution)/shard_map/ppermute | solution.py:37
  51.0 2.9 %collective-permute-start.8 = (bf16[3,64,1024]{2,1,0:T(8,128)(2,1)S(1)}, bf16[3,64,1024]{2,1,0:T(8,128)(2,1)S(1)}, u32[]{:S(2)}, u32[]{:S(2)}) collective-permute-start(bf16[3,64,1024]{2,1,0:T(8,128)(2,1)S(1)} %activation.3.refs_1_), channel_id=1, source_target_pairs={{0,1},{1,0},{2,3},{3,2},{4,5},{5,4},{6,7},{7,6},{8,9},{9,8},{10,11... | collective-permute-start | bytes 1179656 | tf_op jit(solution)/shard_map/ppermute | solution.py:37
  56.5 13.2 %collective-permute-start.9 = (bf16[32,1536]{1,0:T(8,128)(2,1)S(1)}, bf16[32,1536]{1,0:T(8,128)(2,1)S(1)}, u32[]{:S(2)}, u32[]{:S(2)}) collective-permute-start(bf16[32,1536]{1,0:T(8,128)(2,1)S(1)} %get-tuple-element.102), channel_id=1, source_target_pairs={{0,12},{4,0},{8,4},{12,8},{1,13},{5,1},{9,5},{13,9},{2,14},{6,2},{... | collective-permute-start | bytes 294920 | tf_op jit(solution)/shard_map/ppermute | solution.py:37
  58.5 11.2 %collective-permute-start.10 = (bf16[32,1536]{1,0:T(8,128)(2,1)S(1)}, bf16[32,1536]{1,0:T(8,128)(2,1)S(1)}, u32[]{:S(2)}, u32[]{:S(2)}) collective-permute-start(bf16[32,1536]{1,0:T(8,128)(2,1)S(1)} %get-tuple-element.103), channel_id=1, source_target_pairs={{0,8},{4,12},{8,0},{12,4},{1,9},{5,13},{9,1},{13,5},{2,10},{6,14},... | collective-permute-start | bytes 294920 | tf_op jit(solution)/shard_map/ppermute | solution.py:37
  59.3 10.3 %collective-permute-start.11 = (bf16[32,1536]{1,0:T(8,128)(2,1)S(1)}, bf16[32,1536]{1,0:T(8,128)(2,1)S(1)}, u32[]{:S(2)}, u32[]{:S(2)}) collective-permute-start(bf16[32,1536]{1,0:T(8,128)(2,1)S(1)} %get-tuple-element.104), channel_id=1, source_target_pairs={{0,4},{4,8},{8,12},{12,0},{1,5},{5,9},{9,13},{13,1},{2,6},{6,10},{... | collective-permute-start | bytes 294920 | tf_op jit(solution)/shard_map/ppermute | solution.py:37

commit v2 on v1

v2 whole, which is shorter than its diff:
```python
import functools

import jax
import jax.numpy as jnp
from jax import lax
from jax.experimental import pallas as pl
from jax.experimental.pallas import tpu as pltpu
from jax.sharding import PartitionSpec as P

F32 = jnp.float32
BF16 = jnp.bfloat16
CHUNKS = ((4,), (4, 4), (4,))
VMEM_SPEC = pl.BlockSpec(memory_space=pltpu.VMEM)
SMEM_SPEC = pl.BlockSpec(memory_space=pltpu.SMEM)
ANY_SPEC = pl.BlockSpec(memory_space=pl.ANY)
HBM_SPEC = pl.BlockSpec(memory_space=pltpu.MemorySpace.HBM)
LIMIT = 10 << 20
SLOTS = 3


def contract(left, right, left_dim, right_dim):
    return lax.dot_general(
        left, right, (((left_dim,), (right_dim,)), ((), ())), preferred_element_type=F32
    )


def tile_of(width):
    return 256 if width % 256 == 0 else 128


def params(**more):
    return pltpu.CompilerParams(vmem_limit_bytes=LIMIT, **more)


def cost(flops, moved):
    return pl.CostEstimate(flops=int(flops), bytes_accessed=int(moved), transcendentals=0)


def shift(x, axis, size, by):
    return lax.ppermute(x, axis, [(i, (i + by) % size) for i in range(size)])


def column(me_ref, piece):
    start, core, inner, stride, at, _ = piece
    return pl.multiple_of(start + lax.rem(me_ref[0] + core, inner) * stride + at, 128)


def in_vmem(shape, dtype):
    return pltpu.VMEM(shape, dtype)


def in_hbm(x):
    return pltpu.with_memory_space_constraint(x, pltpu.MemorySpace.HBM)


def piece_copies(me, pieces, whole, out, sems):
    copies = []
    for i, piece in enumerate(pieces):
        here = pl.ds(column(me, piece), piece[-1])
        for j in range(3):
            source = whole[j].at[here, :] if j == 2 else whole[j].at[:, here]
            copies.append(pltpu.make_async_copy(source, out[3 * i + j], sems.at[i, j]))
    return copies


def piece_shapes(pieces, features):
    shapes = []
    for piece in pieces:
        shapes += [in_vmem((features, piece[-1]), BF16)] * 2
        shapes += [in_vmem((piece[-1], features), BF16)]
    return shapes


def in_threes(arrays):
    return [tuple(arrays[i : i + 3]) for i in range(0, len(arrays), 3)]


def load_kernel(pieces, me, *refs):
    copies = piece_copies(me, pieces, refs[:3], refs[3:-1], refs[-1])
    for copy in copies:
        copy.start()
    for copy in copies:
        copy.wait()


def load(me, pieces, whole):
    outs = piece_shapes(pieces, whole[0].shape[0])
    moved = 6 * sum(piece[-1] for piece in pieces) * whole[0].shape[0]
    return in_threes(
        pl.pallas_call(
            functools.partial(load_kernel, pieces),
            in_specs=[SMEM_SPEC] + [HBM_SPEC] * 3,
            out_specs=[VMEM_SPEC] * len(outs),
            out_shape=outs,
            scratch_shapes=[pltpu.SemaphoreType.DMA((len(pieces), 3))],
            compiler_params=params(),
            cost_estimate=cost(0, moved),
            name="load_weights",
        )(me, *whole)
    )


def pack_kernel(tokens, cot, packed, sems):
    rows = tokens.shape[0]
    copies = [
        pltpu.make_async_copy(tokens, packed.at[:rows], sems.at[0]),
        pltpu.make_async_copy(cot, packed.at[rows:], sems.at[1]),
    ]
    for copy in copies:
        copy.start()
    for copy in copies:
        copy.wait()


def pack(tokens, cot):
    return pl.pallas_call(
        pack_kernel,
        in_specs=[ANY_SPEC] * 2,
        out_specs=VMEM_SPEC,
        out_shape=in_vmem((2 * tokens.shape[0], tokens.shape[1]), BF16),
        scratch_shapes=[pltpu.SemaphoreType.DMA((2,))],
        compiler_params=params(),
        cost_estimate=cost(0, 8 * tokens.size),
        name="pack_rows",
    )(in_hbm(tokens), in_hbm(cot))


def forward_kernel(rows, pieces, ahead, out_dtype, count, assemble, me, *refs):
    refs = list(refs)
    take = lambda n: [refs.pop(0) for _ in range(n)]
    acts, weights = take(count), in_threes(take(3 * len(pieces)))
    whole = take(3 if ahead else 0)
    (sums,) = take(1)
    tokens_ref, cot_ref = take(2) if assemble else acts
    copies = []
    if ahead:
        out = take(3 * len(ahead))
        copies = piece_copies(me, ahead, whole, out, *take(1))
    for copy in copies:
        copy.start()

    def compute():
        if assemble:
            for k, piece in enumerate(acts):
                tokens_ref[pl.ds(k * rows, rows), :] = piece[:rows, :]
                cot_ref[pl.ds(k * rows, rows), :] = piece[rows:, :]
        tokens, cot = tokens_ref[...], cot_ref[...]
        first = 0
        for (w_gate, w_up, w_down), piece in zip(weights, pieces):
            tile = tile_of(piece[-1])
            for start in range(0, piece[-1], tile):
                here = slice(start, start + tile)
                there = slice(first, first + tile)
                first += tile
                sums[0, :, there] = contract(tokens, w_gate[:, here], 1, 0).astype(out_dtype)
                sums[1, :, there] = contract(tokens, w_up[:, here], 1, 0).astype(out_dtype)
                sums[2, :, there] = contract(cot, w_down[here, :], 1, 1).astype(out_dtype)

    if ahead:
        pl.when(me[0] >= 0)(compute)
    else:
        compute()
    for copy in copies:
        copy.wait()


def forward(me, pieces, acts, weights, rows, out_dtype, ahead, whole):
    assemble = len(acts) != 2
    features = acts[0].shape[1]
    width = sum(piece[-1] for piece in pieces)
    total = rows * len(acts) if assemble else acts[0].shape[0]
    whole = whole if ahead else ()
    outs = [in_vmem((3, total, width), out_dtype)]
    if assemble:
        outs += [in_vmem((total, features), BF16)] * 2
    outs += piece_shapes(ahead, features)
    out = pl.pallas_call(
        functools.partial(
            forward_kernel, rows, pieces, ahead, out_dtype, len(acts), assemble
        ),
        in_specs=[SMEM_SPEC]
        + [VMEM_SPEC] * (len(acts) + 3 * len(pieces))
        + [HBM_SPEC] * len(whole),
        out_specs=[VMEM_SPEC] * len(outs),
        out_shape=outs,
        scratch_shapes=[pltpu.SemaphoreType.DMA((len(ahead), 3))] * bool(ahead),
        compiler_params=params(),
        cost_estimate=cost(6 * total * width, 6 * total * width),
        name="partial_sums",
    )(me, *acts, *(x for three in weights for x in three), *whole)
    loaded = in_threes(out[len(out) - 3 * len(ahead) :]) if ahead else []
    return out[0], out[1:3] if assemble else acts, loaded


def join_kernel(mine, received, kept, sent):
    total = mine[...] + received[...].astype(F32)
    kept[...] = total
    sent[...] = total.astype(BF16)


def join(mine, received):
    return pl.pallas_call(
        join_kernel,
        in_specs=[VMEM_SPEC] * 2,
        out_specs=[VMEM_SPEC] * 2,
        out_shape=[in_vmem(mine.shape, F32), in_vmem(mine.shape, BF16)],
        compiler_params=params(),
        cost_estimate=cost(mine.size, 12 * mine.size),
        name="join_cores",
    )(mine, received)


def activate_kernel(*refs):
    kept, received, out = refs[0], refs[1:-1], refs[-1]
    gate, up, upstream = [
        sum((r[i].astype(F32) for r in received), kept[i]) for i in range(3)
    ]
    sigmoid = 1.0 / (1.0 + jnp.exp(-gate))
    swish = gate * sigmoid
    out[0] = (swish * up).astype(BF16)
    out[1] = (upstream * up * sigmoid * (1.0 + gate * (1.0 - sigmoid))).astype(BF16)
    out[2] = (upstream * swish).astype(BF16)


def activate(kept, received):
    return pl.pallas_call(
        activate_kernel,
        in_specs=[VMEM_SPEC] * (1 + len(received)),
        out_specs=VMEM_SPEC,
        out_shape=in_vmem(kept.shape, BF16),
        compiler_params=params(),
        cost_estimate=cost(8 * kept.size, 8 * kept.size),
        name="activation",
    )(kept, *received)


def backward_kernel(where, rows, grads, first, fresh, last, me, *refs):
    refs = list(refs)
    take = lambda n: [refs.pop(0) for _ in range(n)]
    acts = take(len(where))
    weights = [in_threes(take(3 * len(p))) if rows else [None] * len(p) for p in where]
    tokens, cot = take(2) if grads else (None, None)
    before = take(2) if rows and not first else None
    if grads and not fresh:
        take(3)
    sums = take(1 + last if last else 2) if rows else None
    outs = take(3) if grads else None
    out_acc, grad_acc = (take(2) if last else sums) if rows else (None, None)
    if grads:
        wide, tall, sems = take(3)
    slots = sems.shape[0] if grads else 1

    def copies(slot, at, tile):
        here = pl.ds(at, tile)
        cols = pl.ds(0, tile)
        return [
            pltpu.make_async_copy(
                wide.at[slot, 0, :, cols], outs[0].at[:, here], sems.at[slot, 0]
            ),
            pltpu.make_async_copy(
                wide.at[slot, 1, :, cols], outs[1].at[:, here], sems.at[slot, 1]
            ),
            pltpu.make_async_copy(tall.at[slot, cols], outs[2].at[here, :], sems.at[slot, 2]),
        ]

    if rows:
        if first:
            out_acc[...] = jnp.zeros_like(out_acc)
            grad_acc[...] = jnp.zeros_like(grad_acc)
        else:
            out_acc[...] = before[0][...]
            grad_acc[...] = before[1][...]
    flying, tiles = [], []
    for p, pieces in enumerate(where):
        done = 0
        for three, piece in zip(weights[p], pieces):
            tile = tile_of(piece[-1])
            for at in range(0, piece[-1], tile):
                tiles.append((p, slice(done + at, done + at + tile), three, piece, at))
            done += piece[-1]

    def make_grads(p, units, _, piece, at):
        hidden, grad_gate, grad_up = [acts[p][i, :, units] for i in range(3)]
        slot, tile = len(flying) % slots, units.stop - units.start
        if len(flying) >= slots:
            for copy in flying[len(flying) - slots]:
                copy.wait()
        cols = slice(0, tile)
        wide[slot, 0, :, cols] = contract(tokens[...], grad_gate, 0, 0).astype(BF16)
        wide[slot, 1, :, cols] = contract(tokens[...], grad_up, 0, 0).astype(BF16)
        tall[slot, cols] = contract(hidden, cot[...], 0, 0).astype(BF16)
        flying.append(copies(slot, pl.multiple_of(column(me, piece) + at, 128), tile))
        for copy in flying[-1]:
            copy.start()

    def add_rows(p, units, three, piece, at):
        hidden, grad_gate, grad_up = [acts[p][i, :, units] for i in range(3)]
        w_gate, w_up, w_down = three
        here = slice(at, at + units.stop - units.start)
        out_acc[...] += contract(hidden, w_down[here, :], 1, 0)
        grad_acc[...] += contract(grad_gate, w_gate[:, here], 1, 1) + contract(
            grad_up, w_up[:, here], 1, 1
        )

    behind = 2 if grads else 0
    for i in range(len(tiles) + behind):
        if grads and i < len(tiles) and tiles[i][0] in grads:
            make_grads(*tiles[i])
        if rows and i >= behind:
            add_rows(*tiles[i - behind])
    if last:
        n = sums[0].shape[0] // 2
        for k, ref in enumerate(sums):
            ref[:n, :] = out_acc[k * n : (k + 1) * n, :].astype(ref.dtype)
            ref[n:, :] = grad_acc[k * n : (k + 1) * n, :].astype(ref.dtype)
    for group in flying[-slots:]:
        for copy in group:
            copy.wait()


def backward(
    me, where, acts, weights, tokens, cot, before, grads, hidden, last_rows=0, of=None
):
    total = acts[0].shape[1]
    features = tokens.shape[1]
    width = sum(a.shape[2] for a in acts)
    rows, makes = before is not None, grads is not None
    args, specs, outs, out_specs, scratch = [me, *acts], [], [], [], []
    if rows:
        args += [x for part in weights for three in part for x in three]
    if makes:
        args += [tokens, cot]
    if rows:
        args += before
    specs = [SMEM_SPEC] + [VMEM_SPEC] * (len(args) - 1)
    aliases = {}
    if rows:
        if last_rows:
            shape = (2 * last_rows, features)
            outs += [in_vmem(shape, F32)] + [in_vmem(shape, BF16)] * (total // last_rows - 1)
            scratch += [pltpu.VMEM((total, features), F32)] * 2
        else:
            outs += [in_vmem((total, features), F32)] * 2
        out_specs += [VMEM_SPEC] * len(outs)
    if makes:
        aliases = {len(args) + i: len(outs) + i for i in range(len(grads))}
        args += grads
        specs += [HBM_SPEC] * len(grads)
        outs += [
            pltpu.HBM((features, hidden), BF16),
            pltpu.HBM((features, hidden), BF16),
            pltpu.HBM((hidden, features), BF16),
        ]
        out_specs += [HBM_SPEC] * 3
        tile = max(tile_of(piece[-1]) for part in where for piece in part)
        scratch += [
            pltpu.VMEM((SLOTS, 2, features, tile), BF16),
            pltpu.VMEM((SLOTS, tile, features), BF16),
            pltpu.SemaphoreType.DMA((SLOTS, 3)),
        ]
    work = width * features * (rows + makes)
    out = pl.pallas_call(
        functools.partial(
            backward_kernel, where, rows, of or range(len(where)) if makes else (), not before, not grads,
            total // last_rows - 1 if last_rows else 0,
        ),
        in_specs=specs,
        out_specs=out_specs,
        out_shape=outs,
        scratch_shapes=scratch,
        input_output_aliases=aliases,
        compiler_params=params(),
        cost_estimate=cost(6 * total * work, 6 * work),
        name="output_rows" if not makes else "weight_grads" if not rows else "backward",
    )(*args)
    return (out[:-3], out[-3:]) if makes else (out, None)


def finish_kernel(*refs):
    mine, received, (output, grad_input) = refs[0], refs[1:-2], refs[-2:]
    rows = output.shape[0]
    total = mine[...]
    for r in received:
        total = total + r[...].astype(F32)
    output[...] = total[:rows].astype(BF16)
    grad_input[...] = total[rows:].astype(BF16)


def finish(mine, received):
    shape = jax.ShapeDtypeStruct((mine.shape[0] // 2, mine.shape[1]), BF16)
    return pl.pallas_call(
        finish_kernel,
        in_specs=[VMEM_SPEC] * (1 + len(received)),
        out_specs=[VMEM_SPEC] * 2,
        out_shape=[shape] * 2,
        compiler_params=params(),
        name="finish_rows",
    )(mine, *received)


def chunk_parts(hidden, inner):
    units = hidden // inner
    if units % 2048 == 0:
        chunks = [[units * share // 16 for share in chunk] for chunk in CHUNKS]
    else:
        chunks = [[units // 2]] * 2 if units % 256 == 0 else [[units]]
    parts, start = [], 0
    for widths in chunks:
        stride = sum(widths)
        parts.append([
            [(start, core, inner, stride, sum(widths[:i]), w) for i, w in enumerate(widths)]
            for core in range(inner)
        ])
        start += inner * stride
    return parts


def tied(acts, held):
    acts, arrays = lax.optimization_barrier((acts, list(held.values())))
    return acts, dict(zip(held, arrays))


def body(sizes, tokens, cotangent, w_gate, w_up, w_down):
    wide, narrow, inner = sizes["wide"], sizes["narrow"], sizes["inner"]
    rows = tokens.shape[0]
    hidden = w_gate.shape[1]
    me = lax.axis_index("inner").astype(jnp.int32).reshape(1)
    parts = chunk_parts(hidden, inner)
    whole = tuple(in_hbm(w) for w in (w_gate, w_up, w_down))

    packed = pack(tokens, cotangent)
    acts = [packed] + [shift(packed, "wide", wide, k) for k in range(1, wide)]
    uses = [pieces for mine, other in parts for pieces in (other, mine)]
    queue = [piece for pieces in uses for piece in pieces]
    plan, seen = [[]], 0
    while queue and (not plan[0] or 2 * (seen + queue[0][-1]) <= hidden):
        seen += queue[0][-1]
        plan[0].append(queue.pop(0))
    for i in range(len(uses)):
        plan.append([queue.pop(0)] if queue else [])
        while queue and i + 1 < len(uses) and queue[0] in uses[i + 1]:
            plan[-1].append(queue.pop(0))
    held = dict(zip(plan[0], load(me, plan[0], whole)))
    acts, held = tied(acts, held)
    kept, products, crossed = [], [], []
    step = 1
    for mine, other in parts:
        made = []
        for pieces, dtype in ((other, BF16), (mine, F32)):
            weights = [held[piece] for piece in pieces]
            out, acts, loaded = forward(
                me, pieces, acts, weights, rows, dtype, plan[step], whole
            )
            held.update(zip(plan[step], loaded))
            step += 1
            made.append(out)
        products.append(made)
        total, out = join(made[1], shift(made[0], "inner", inner, 1))
        acts, _ = lax.optimization_barrier((acts, out))
        kept.append(total)
        crossed.append([shift(out, "narrow", narrow, k) for k in range(1, narrow)])
    tokens_all, cot_all = acts
    crossed[0], _ = lax.optimization_barrier((crossed[0], products[-1]))
    sums, grads, later = (), (), []
    for i, where in enumerate(parts):
        own = activate(kept[i], crossed[i])
        acts = [own, shift(own, "inner", inner, 1)]
        weights = [[held[piece] for piece in pieces] for pieces in where]
        if where is parts[-1]:
            later += list(zip(where, acts))
        else:
            of = (0, 1)
            if i == len(parts) - 2 and i:
                of, later = (0,), [(where[1], acts[1])]
            sums, grads = backward(
                me, where, acts, weights, tokens_all, cot_all, sums, grads, hidden, of=of
            )
            crossed[i + 1], sums = lax.optimization_barrier((crossed[i + 1], sums))
    for last, (pieces, act, three) in enumerate(zip(where, acts, weights)):
        sums, _ = backward(
            me, [pieces], [act], [three], tokens_all, cot_all, sums, None, hidden,
            rows if last else 0,
        )
    back = [shift(sums[k], "wide", wide, -k) for k in range(1, wide)]
    where, acts = zip(*later)
    _, grads = backward(me, where, acts, None, tokens_all, cot_all, None, grads, hidden)
    output, grad_input = finish(sums[0], back)
    return (output, grad_input, *grads)


def solution(mesh):
    rows = P(("groups", "wide"), ("narrow", "inner"))
    return jax.shard_map(
        functools.partial(body, dict(mesh.shape)),
        mesh=mesh,
        in_specs=(
            rows,
            rows,
            P(("narrow", "inner"), "wide"),
            P(("narrow", "inner"), "wide"),
            P("wide", ("narrow", "inner")),
        ),
        out_specs=(
            rows,
            rows,
            P(("groups", "narrow", "inner"), "wide"),
            P(("groups", "narrow", "inner"), "wide"),
            P(("groups", "wide"), ("narrow", "inner")),
        ),
        check_vma=False,
    )
```

time: 70.6 us -> 65 us (0.921)
  waiting for transfers between devices: 8.59 us -> 3.41 us
  local copies, waits for them, and re-layouts: 1.59 us -> 0 us
  starting transfers between devices: 14.4 us -> 15.7 us
    ppermute x12 -> x15, waiting for transfers between devices: 8.59 us -> 3.41 us  [shift(): return lax.ppermute(x, axis, [(i, (i + by) % size) for i in range(size)])]
    unnamed x4 -> x0, local copies, waits for them, and re-layouts: 1.59 us -> none
    ppermute x12 -> x15, starting transfers between devices: 14.4 us -> 15.7 us  [shift(): return lax.ppermute(x, axis, [(i, (i + by) % size) for i in range(size)])]
    pallas_call x10 -> x13, Pallas kernels: 43.6 us -> 43.6 us  [the longest x5 24.3 us: backward(): pl.pallas_call(functools.partial(backward_kernel, where, rows, of or rang...]
  transfers between devices with their start and end apart: 12 -> 15, of which waited for: 3 -> 5; matrix products, arithmetic and copies ran while one was open for 0% -> 0% of each run, Pallas kernels for 50% -> 57%
where the time goes in v2:
time: 65 us; the launch traced here: 64.8 us
  Pallas kernels  44.9 us (69%)
  starting transfers between devices  15.7 us (24%)
  waiting for transfers between devices  3.41 us (5%)
  between operations  0.83 us (1%)
    pallas_call x5, Pallas kernels, backward(): pl.pallas_call(functools.partial(backward_kernel, where, rows, of or rang...  24.3 us
    ppermute x15, starting transfers between devices, shift(): return lax.ppermute(x, axis, [(i, (i + by) % size) for i in range(size)])  15.7 us
    pallas_call x6, Pallas kernels, forward(): pl.pallas_call(functools.partial(forward_kernel, rows, pieces, ahead, out...  11.9 us
    pallas_call x1, Pallas kernels, load(): pl.pallas_call(functools.partial(load_kernel, pieces), in_specs=[SMEM_SPE...  6.62 us
    ppermute x15, waiting for transfers between devices, shift(): return lax.ppermute(x, axis, [(i, (i + by) % size) for i in range(size)])  3.41 us
  transfers between devices with their start and end apart: 15, of which 5 were waited for; matrix products, arithmetic and copies ran while one was open for 0% of the time, Pallas kernels for 57%

profile of v2, /device:TPU:0, one launch (start us, length us, event | category | flops | bytes accessed | tf_op | source)
XLA Modules:
  0.0 64.8 jit_solution(8890991945697360133)
XLA Ops:
  0.6 0.8 %pack_rows.1.refs_0_ = bf16[32,1536]{1,0:T(8,128)(2,1)S(1)} custom-call(bf16[16,1536]{1,0:T(8,128)(2,1)} %tokens.1, bf16[16,1536]{1,0:T(8,128)(2,1)} %cot.1), custom_call_target="tpu_custom_call" | custom-call | bytes 196608 | tf_op jit(solution)/shard_map/pack_rows/pallas_call | solution.py:116
  1.5 5.1 %collective-permute-start.2 = (bf16[32,1536]{1,0:T(8,128)(2,1)S(1)}, bf16[32,1536]{1,0:T(8,128)(2,1)S(1)}, u32[]{:S(2)}, u32[]{:S(2)}) collective-permute-start(bf16[32,1536]{1,0:T(8,128)(2,1)S(1)} %pack_rows.1.refs_0_), channel_id=1, source_target_pairs={{0,12},{4,0},{8,4},{12,8},{1,13},{5,1},{9,5},{13,9},{2,14},{6,2},{... | collective-permute-start | bytes 294920 | tf_op jit(solution)/shard_map/ppermute | solution.py:40
  6.6 0.0 collective-permute-start.1
  6.6 1.0 %collective-permute-start = (bf16[32,1536]{1,0:T(8,128)(2,1)S(1)}, bf16[32,1536]{1,0:T(8,128)(2,1)S(1)}, u32[]{:S(2)}, u32[]{:S(2)}) collective-permute-start(bf16[32,1536]{1,0:T(8,128)(2,1)S(1)} %pack_rows.1.refs_0_), channel_id=1, source_target_pairs={{0,4},{4,8},{8,12},{12,0},{1,5},{5,9},{9,13},{13,1},{2,6},{6,10},{... | collective-permute-start | bytes 294920 | tf_op jit(solution)/shard_map/ppermute | solution.py:40
  7.6 6.6 %load_weights.1 = (bf16[1536,512]{1,0:T(8,128)(2,1)S(1)}, bf16[1536,512]{1,0:T(8,128)(2,1)S(1)}, bf16[512,1536]{1,0:T(8,128)(2,1)S(1)}, bf16[1536,512]{1,0:T(8,1...) custom-call(s32[1]{0:T(128)} %bitcast.me, ...), custom_call_target="tpu_custom_call" | custom-call | bytes 18874368 | tf_op jit(solution)/shard_map/load_weights/pallas_call | solution.py:90
  14.2 0.0 collective-permute-done.2.refs_3_
  14.2 1.1 %collective-permute-done.1.refs_2_ = bf16[32,1536]{1,0:T(8,128)(2,1)S(1)} collective-permute-done((bf16[32,1536]{1,0:T(8,128)(2,1)S(1)}, bf16[32,1536]{1,0:T(8,128)(2,1)S(1)}, u32[]{:S(2)}, u32[]{:S(2)}) %collective-permute-start.1) | collective-permute-done | bytes 98336 | tf_op jit(solution)/shard_map/ppermute | solution.py:40
  15.3 0.0 collective-permute-done.refs_1_
  15.3 2.4 %partial_sums.6 = (bf16[3,64,512]{2,1,0:T(8,128)(2,1)S(1)}, bf16[64,1536]{1,0:T(8,128)(2,1)S(1)}, bf16[64,1536]{1,0:T(8,128)(2,1)S(1)}, bf16[1536,512]{1,0:T(8,1...) custom-call(s32[1]{0:T(128)} %bitcast.me, bf16[32,1536]{1,0:T(8,128)(2,1)S(1)} %pack_rows.1.refs_0_, ...), custom_call_target="tpu_custom_call" | custom-call | flops 196608 | bytes 196608 | tf_op jit(solution)/shard_map/partial_sums/pallas_call | solution.py:177
  17.7 0.1 collective-permute-start.3
  17.8 2.4 %partial_sums.7 = (f32[3,64,512]{2,1,0:T(8,128)S(1)}, bf16[1536,512]{1,0:T(8,128)(2,1)S(1)}, bf16[1536,512]{1,0:T(8,128)(2,1)S(1)}, bf16[512,1536]{1,0:T(8,128)(2,1)S(1)}) custom-call(s32[1]{0:T(128)} %bitcast.me, bf16[64,1536]{1,0:T(8,128)(2,1)S(1)} %get-tuple-element.148.refs_0_.refs_8_.refs_14_.refs_3_, ...), custom_call_target="tpu_custom_call" | custom-call | flops 196608 | bytes 196608 | tf_op jit(solution)/shard_map/partial_sums/pallas_call | solution.py:177
  20.3 0.1 join_cores.3
  20.3 2.4 %partial_sums.9 = (bf16[3,64,1024]{2,1,0:T(8,128)(2,1)S(1)}, bf16[1536,512]{1,0:T(8,128)(2,1)S(1)}, bf16[1536,512]{1,0:T(8,128)(2,1)S(1)}, bf16[512,1536]{1,0:T(8,128)(2,1)S(1)}) custom-call(s32[1]{0:T(128)} %bitcast.me, bf16[64,1536]{1,0:T(8,128)(2,1)S(1)} %get-tuple-element.148.refs_0_.refs_8_.refs_14_.refs_3_, ...), custom_call_target="tpu_custom_call" | custom-call | flops 393216 | bytes 393216 | tf_op jit(solution)/shard_map/partial_sums/pallas_call | solution.py:177
  22.8 0.6 collective-permute-start.4
  23.3 1.5 %collective-permute-start.8 = (bf16[3,64,512]{2,1,0:T(8,128)(2,1)S(1)}, bf16[3,64,512]{2,1,0:T(8,128)(2,1)S(1)}, u32[]{:S(2)}, u32[]{:S(2)}) collective-permute-start(bf16[3,64,512]{2,1,0:T(8,128)(2,1)S(1)} %get-tuple-element.117), channel_id=1, source_target_pairs={{0,2},{2,0},{1,3},{3,1},{4,6},{6,4},{5,7},{7,5},{8,10},{10,8},{9,1... | collective-permute-start | bytes 589832 | tf_op jit(solution)/shard_map/ppermute | solution.py:40
  24.8 2.4 %partial_sums.8 = (f32[3,64,1024]{2,1,0:T(8,128)S(1)}, bf16[1536,512]{1,0:T(8,128)(2,1)S(1)}, bf16[1536,512]{1,0:T(8,128)(2,1)S(1)}, bf16[512,1536]{1,0:T(8,128)(2,1)S(1)}) custom-call(s32[1]{0:T(128)} %bitcast.me, bf16[64,1536]{1,0:T(8,128)(2,1)S(1)} %get-tuple-element.148.refs_0_.refs_8_.refs_14_.refs_3_, ...), custom_call_target="tpu_custom_call" | custom-call | flops 393216 | bytes 393216 | tf_op jit(solution)/shard_map/partial_sums/pallas_call | solution.py:177
  27.2 0.0 collective-permute-done.4.received
  27.2 0.1 join_cores.4
  27.3 0.6 collective-permute-start.7
  27.9 1.1 %partial_sums.11 = bf16[3,64,512]{2,1,0:T(8,128)(2,1)S(1)} custom-call(s32[1]{0:T(128)} %bitcast.me, bf16[64,1536]{1,0:T(8,128)(2,1)S(1)} %get-tuple-element.148.refs_0_.refs_8_.refs_14_.refs_3_, bf16[64,1536]{1,0:T(8,128)(2,1)S(1)} %get-tuple-element.149.refs_1_.refs_9_.refs_15_.refs_4_, bf16[1536,512]{1,0:T(8,128)(2,1)S(1)} %get-tuple-element.140.refs_2_.refs_1_, ...), custom_call_target="tpu_custom_call" | custom-call | flops 196608 | bytes 196608 | tf_op jit(solution)/shard_map/partial_sums/pallas_call | solution.py:177
  29.1 0.1 collective-permute-start.5
  29.1 1.1 %partial_sums.10.mine = f32[3,64,512]{2,1,0:T(8,128)S(1)} custom-call(s32[1]{0:T(128)} %bitcast.me, bf16[64,1536]{1,0:T(8,128)(2,1)S(1)} %get-tuple-element.148.refs_0_.refs_8_.refs_14_.refs_3_, bf16[64,1536]{1,0:T(8,128)(2,1)S(1)} %get-tuple-element.149.refs_1_.refs_9_.refs_15_.refs_4_, bf16[1536,512]{1,0:T(8,128)(2,1)S(1)} %get-tuple-element.137.refs_2_.refs_1_, ...), custom_call_target="tpu_custom_call" | custom-call | flops 196608 | bytes 196608 | tf_op jit(solution)/shard_map/partial_sums/pallas_call | solution.py:177
  30.3 0.2 collective-permute-done.8.refs_1_
  30.5 0.1 activation.3.refs_0_
  30.6 0.3 collective-permute-start.9
  31.0 0.0 collective-permute-done.5.received
  31.0 0.1 join_cores.5
  31.0 1.1 %collective-permute-done.9.refs_1_ = bf16[3,64,512]{2,1,0:T(8,128)(2,1)S(1)} collective-permute-done((bf16[3,64,512]{2,1,0:T(8,128)(2,1)S(1)}, bf16[3,64,512]{2,1,0:T(8,128)(2,1)S(1)}, u32[]{:S(2)}, u32[]{:S(2)}) %collective-permute-start.9) | collective-permute-done | bytes 196640 | tf_op jit(solution)/shard_map/ppermute | solution.py:40
  32.1 6.2 %backward.2 = (f32[64,1536]{1,0:T(8,128)S(1)}, f32[64,1536]{1,0:T(8,128)S(1)}, bf16[1536,4096]{1,0:T(8,128)(2,1)}, bf16[1536,4096]{1,0:T(8,128)(2,1)}, bf16[4096,1536]{1,0:T(8,128)(2,1)}) custom-call(s32[1]{0:T(128)} %bitcast.me, bf16[3,64,512]{2,1,0:T(8,128)(2,1)S(1)} %activation.3.refs_0_, bf16[3,64,512]{2,1,0:T(8,128)(2,1)S(1)} %collective-permute-done.9.refs_1_, ...), custom_call_target="tpu_custom_call" | custom-call | flops 1207959552 | bytes 18874368 | tf_op jit(solution)/shard_map/backward/pallas_call | solution.py:362
  38.3 0.3 collective-permute-done.7.refs_1_
  38.6 0.2 activation.4.refs_0_
  38.8 0.1 collective-permute-start.10
  38.9 1.9 %collective-permute-start.6 = (bf16[3,64,512]{2,1,0:T(8,128)(2,1)S(1)}, bf16[3,64,512]{2,1,0:T(8,128)(2,1)S(1)}, u32[]{:S(2)}, u32[]{:S(2)}) collective-permute-start(bf16[3,64,512]{2,1,0:T(8,128)(2,1)S(1)} %get-tuple-element.144), channel_id=1, source_target_pairs={{0,2},{2,0},{1,3},{3,1},{4,6},{6,4},{5,7},{7,5},{8,10},{10,8},{9,1... | collective-permute-start | bytes 589832 | tf_op jit(solution)/shard_map/ppermute | solution.py:40
  40.8 0.0 collective-permute-done.10.refs_1_.refs_0_
  40.8 8.0 %backward.3 = (f32[64,1536]{1,0:T(8,128)S(1)}, f32[64,1536]{1,0:T(8,128)S(1)}, bf16[1536,4096]{1,0:T(8,128)(2,1)}, bf16[1536,4096]{1,0:T(8,128)(2,1)}, bf16[4096,1536]{1,0:T(8,128)(2,1)}) custom-call(s32[1]{0:T(128)} %bitcast.me, bf16[3,64,1024]{2,1,0:T(8,128)(2,1)S(1)} %activation.4.refs_0_, ...), custom_call_target="tpu_custom_call", output_to_operand_aliasing={{2}: (19, {}), {3}: (20, {}), {4}: (21, {})} | custom-call | flops 2415919104 | bytes 37748736 | tf_op jit(solution)/shard_map/backward/pallas_call | solution.py:362
  48.9 0.1 activation.5.refs_0_.refs_1_
  49.0 0.1 collective-permute-start.11
  49.1 1.3 %output_rows.2 = (f32[64,1536]{1,0:T(8,128)S(1)}, f32[64,1536]{1,0:T(8,128)S(1)}) custom-call(s32[1]{0:T(128)} %bitcast.me, bf16[3,64,512]{2,1,0:T(8,128)(2,1)S(1)} %activation.5.refs_0_.refs_1_, bf16[1536,512]{1,0:T(8,128)(2,1)S(1)} %get-tuple-element.137.refs_2_.refs_1_, bf16[1536,512]{1,0:T(8,128)(2,1)S(1)} %get-tuple-element.138.refs_3_.refs_2_, ...), custom_call_target="tpu_custom_call" | custom-call | flops 301989888 | bytes 4718592 | tf_op jit(solution)/shard_map/output_rows/pallas_call | solution.py:362
  50.5 0.0 collective-permute-done.11.refs_0_.refs_2_
  50.5 1.3 %output_rows.3 = (f32[32,1536]{1,0:T(8,128)S(1)}, bf16[32,1536]{1,0:T(8,128)(2,1)S(1)}, bf16[32,1536]{1,0:T(8,128)(2,1)S(1)}, bf16[32,1536]{1,0:T(8,128)(2,1)S(1)}) custom-call(s32[1]{0:T(128)} %bitcast.me, bf16[3,64,512]{2,1,0:T(8,128)(2,1)S(1)} %collective-permute-done.11.refs_0_.refs_2_, bf16[1536,512]{1,0:T(8,128)(2,1)S(1)} %get-tuple-element.140.refs_2_.refs_1_, ...), custom_call_target="tpu_custom_call" | custom-call | flops 301989888 | bytes 4718592 | tf_op jit(solution)/shard_map/output_rows/pallas_call | solution.py:362
  51.8 2.0 %collective-permute-start.12 = (bf16[32,1536]{1,0:T(8,128)(2,1)S(1)}, bf16[32,1536]{1,0:T(8,128)(2,1)S(1)}, u32[]{:S(2)}, u32[]{:S(2)}) collective-permute-start(bf16[32,1536]{1,0:T(8,128)(2,1)S(1)} %get-tuple-element.166), channel_id=1, source_target_pairs={{0,12},{4,0},{8,4},{12,8},{1,13},{5,1},{9,5},{13,9},{2,14},{6,2},{... | collective-permute-start | bytes 294920 | tf_op jit(solution)/shard_map/ppermute | solution.py:40
  53.8 0.9 %collective-permute-start.13 = (bf16[32,1536]{1,0:T(8,128)(2,1)S(1)}, bf16[32,1536]{1,0:T(8,128)(2,1)S(1)}, u32[]{:S(2)}, u32[]{:S(2)}) collective-permute-start(bf16[32,1536]{1,0:T(8,128)(2,1)S(1)} %get-tuple-element.167), channel_id=1, source_target_pairs={{0,8},{4,12},{8,0},{12,4},{1,9},{5,13},{9,1},{13,5},{2,10},{6,14},... | collective-permute-start | bytes 294920 | tf_op jit(solution)/shard_map/ppermute | solution.py:40
  54.7 1.4 %collective-permute-start.14 = (bf16[32,1536]{1,0:T(8,128)(2,1)S(1)}, bf16[32,1536]{1,0:T(8,128)(2,1)S(1)}, u32[]{:S(2)}, u32[]{:S(2)}) collective-permute-start(bf16[32,1536]{1,0:T(8,128)(2,1)S(1)} %get-tuple-element.168), channel_id=1, source_target_pairs={{0,4},{4,8},{8,12},{12,0},{1,5},{5,9},{9,13},{13,1},{2,6},{6,10},{... | collective-permute-start | bytes 294920 | tf_op jit(solution)/shard_map/ppermute | solution.py:40
  56.2 7.4 %weight_grads.1 = (bf16[1536,4096]{1,0:T(8,128)(2,1)}, bf16[1536,4096]{1,0:T(8,128)(2,1)}, bf16[4096,1536]{1,0:T(8,128)(2,1)}) custom-call(s32[1]{0:T(128)} %bitcast.me, bf16[3,64,1024]{2,1,0:T(8,128)(2,1)S(1)} %collective-permute-done.10.refs_1_.refs_0_, ...), custom_call_target="tpu_custom_call", output_to_operand_aliasing={{0}: (6, {}), {1}: (7, {}), {2}: (8, {})} | custom-call | flops 1207959552 | bytes 18874368 | tf_op jit(solution)/shard_map/weight_grads/pallas_call | solution.py:362
  63.5 0.0 collective-permute-done.12.refs_1_
  63.6 0.6 collective-permute-done.13.refs_2_
  64.2 0.0 collective-permute-done.14.refs_3_
  64.2 0.7 %finish_rows.1 = (bf16[16,1536]{1,0:T(8,128)(2,1)}, bf16[16,1536]{1,0:T(8,128)(2,1)}) custom-call(f32[32,1536]{1,0:T(8,128)S(1)} %get-tuple-element.165.refs_0_, bf16[32,1536]{1,0:T(8,128)(2,1)S(1)} %collective-permute-done.12.refs_1_, bf16[32,1536]{1,0:T(8,128)(2,1)S(1)} %collective-permute-done.13.refs_2_, bf16[32,1536]{1,0:T(8,128)(2,1)S(1)} %collective-permute-done.14.refs_3_), custom_call_target="tpu_custom_call" | custom-call | tf_op jit(solution)/shard_map/finish_rows/pallas_call | solution.py:391
  (2 shorter events, 0.0 us)
Async XLA Ops:
  1.5 12.8 %collective-permute-start.2 = (bf16[32,1536]{1,0:T(8,128)(2,1)S(1)}, bf16[32,1536]{1,0:T(8,128)(2,1)S(1)}, u32[]{:S(2)}, u32[]{:S(2)}) collective-permute-start(bf16[32,1536]{1,0:T(8,128)(2,1)S(1)} %pack_rows.1.refs_0_), channel_id=1, source_target_pairs={{0,12},{4,0},{8,4},{12,8},{1,13},{5,1},{9,5},{13,9},{2,14},{6,2},{... | collective-permute-start | bytes 294920 | tf_op jit(solution)/shard_map/ppermute | solution.py:40
  6.6 8.7 %collective-permute-start.1 = (bf16[32,1536]{1,0:T(8,128)(2,1)S(1)}, bf16[32,1536]{1,0:T(8,128)(2,1)S(1)}, u32[]{:S(2)}, u32[]{:S(2)}) collective-permute-start(bf16[32,1536]{1,0:T(8,128)(2,1)S(1)} %pack_rows.1.refs_0_), channel_id=1, source_target_pairs={{0,8},{4,12},{8,0},{12,4},{1,9},{5,13},{9,1},{13,5},{2,10},{6,14},... | collective-permute-start | bytes 294920 | tf_op jit(solution)/shard_map/ppermute | solution.py:40
  6.6 8.7 %collective-permute-start = (bf16[32,1536]{1,0:T(8,128)(2,1)S(1)}, bf16[32,1536]{1,0:T(8,128)(2,1)S(1)}, u32[]{:S(2)}, u32[]{:S(2)}) collective-permute-start(bf16[32,1536]{1,0:T(8,128)(2,1)S(1)} %pack_rows.1.refs_0_), channel_id=1, source_target_pairs={{0,4},{4,8},{8,12},{12,0},{1,5},{5,9},{9,13},{13,1},{2,6},{6,10},{... | collective-permute-start | bytes 294920 | tf_op jit(solution)/shard_map/ppermute | solution.py:40
  17.7 2.5 %collective-permute-start.3 = (bf16[3,64,512]{2,1,0:T(8,128)(2,1)S(1)}, bf16[3,64,512]{2,1,0:T(8,128)(2,1)S(1)}, u32[]{:S(2)}, u32[]{:S(2)}) collective-permute-start(bf16[3,64,512]{2,1,0:T(8,128)(2,1)S(1)} %get-tuple-element.116), channel_id=1, source_target_pairs={{0,1},{1,0},{2,3},{3,2},{4,5},{5,4},{6,7},{7,6},{8,9},{9,8},{10,11... | collective-permute-start | bytes 589832 | tf_op jit(solution)/shard_map/ppermute | solution.py:40
  22.8 4.5 %collective-permute-start.4 = (bf16[3,64,1024]{2,1,0:T(8,128)(2,1)S(1)}, bf16[3,64,1024]{2,1,0:T(8,128)(2,1)S(1)}, u32[]{:S(2)}, u32[]{:S(2)}) collective-permute-start(bf16[3,64,1024]{2,1,0:T(8,128)(2,1)S(1)} %get-tuple-element.133), channel_id=1, source_target_pairs={{0,1},{1,0},{2,3},{3,2},{4,5},{5,4},{6,7},{7,6},{8,9},{9,8},{10,11... | collective-permute-start | bytes 1179656 | tf_op jit(solution)/shard_map/ppermute | solution.py:40
  23.3 7.2 %collective-permute-start.8 = (bf16[3,64,512]{2,1,0:T(8,128)(2,1)S(1)}, bf16[3,64,512]{2,1,0:T(8,128)(2,1)S(1)}, u32[]{:S(2)}, u32[]{:S(2)}) collective-permute-start(bf16[3,64,512]{2,1,0:T(8,128)(2,1)S(1)} %get-tuple-element.117), channel_id=1, source_target_pairs={{0,2},{2,0},{1,3},{3,1},{4,6},{6,4},{5,7},{7,5},{8,10},{10,8},{9,1... | collective-permute-start | bytes 589832 | tf_op jit(solution)/shard_map/ppermute | solution.py:40
  27.3 11.3 %collective-permute-start.7 = (bf16[3,64,1024]{2,1,0:T(8,128)(2,1)S(1)}, bf16[3,64,1024]{2,1,0:T(8,128)(2,1)S(1)}, u32[]{:S(2)}, u32[]{:S(2)}) collective-permute-start(bf16[3,64,1024]{2,1,0:T(8,128)(2,1)S(1)} %get-tuple-element.134), channel_id=1, source_target_pairs={{0,2},{2,0},{1,3},{3,1},{4,6},{6,4},{5,7},{7,5},{8,10},{10,8},{9,1... | collective-permute-start | bytes 1179656 | tf_op jit(solution)/shard_map/ppermute | solution.py:40
  29.1 1.9 %collective-permute-start.5 = (bf16[3,64,512]{2,1,0:T(8,128)(2,1)S(1)}, bf16[3,64,512]{2,1,0:T(8,128)(2,1)S(1)}, u32[]{:S(2)}, u32[]{:S(2)}) collective-permute-start(bf16[3,64,512]{2,1,0:T(8,128)(2,1)S(1)} %partial_sums.11), channel_id=1, source_target_pairs={{0,1},{1,0},{2,3},{3,2},{4,5},{5,4},{6,7},{7,6},{8,9},{9,8},{10,11... | collective-permute-start | bytes 589832 | tf_op jit(solution)/shard_map/ppermute | solution.py:40
  30.6 1.5 %collective-permute-start.9 = (bf16[3,64,512]{2,1,0:T(8,128)(2,1)S(1)}, bf16[3,64,512]{2,1,0:T(8,128)(2,1)S(1)}, u32[]{:S(2)}, u32[]{:S(2)}) collective-permute-start(bf16[3,64,512]{2,1,0:T(8,128)(2,1)S(1)} %activation.3.refs_0_), channel_id=1, source_target_pairs={{0,1},{1,0},{2,3},{3,2},{4,5},{5,4},{6,7},{7,6},{8,9},{9,8},{10,11... | collective-permute-start | bytes 589832 | tf_op jit(solution)/shard_map/ppermute | solution.py:40
  38.8 2.0 %collective-permute-start.10 = (bf16[3,64,1024]{2,1,0:T(8,128)(2,1)S(1)}, bf16[3,64,1024]{2,1,0:T(8,128)(2,1)S(1)}, u32[]{:S(2)}, u32[]{:S(2)}) collective-permute-start(bf16[3,64,1024]{2,1,0:T(8,128)(2,1)S(1)} %activation.4.refs_0_), channel_id=1, source_target_pairs={{0,1},{1,0},{2,3},{3,2},{4,5},{5,4},{6,7},{7,6},{8,9},{9,8},{10,11... | collective-permute-start | bytes 1179656 | tf_op jit(solution)/shard_map/ppermute | solution.py:40
  38.9 10.0 %collective-permute-start.6 = (bf16[3,64,512]{2,1,0:T(8,128)(2,1)S(1)}, bf16[3,64,512]{2,1,0:T(8,128)(2,1)S(1)}, u32[]{:S(2)}, u32[]{:S(2)}) collective-permute-start(bf16[3,64,512]{2,1,0:T(8,128)(2,1)S(1)} %get-tuple-element.144), channel_id=1, source_target_pairs={{0,2},{2,0},{1,3},{3,1},{4,6},{6,4},{5,7},{7,5},{8,10},{10,8},{9,1... | collective-permute-start | bytes 589832 | tf_op jit(solution)/shard_map/ppermute | solution.py:40
  49.0 1.5 %collective-permute-start.11 = (bf16[3,64,512]{2,1,0:T(8,128)(2,1)S(1)}, bf16[3,64,512]{2,1,0:T(8,128)(2,1)S(1)}, u32[]{:S(2)}, u32[]{:S(2)}) collective-permute-start(bf16[3,64,512]{2,1,0:T(8,128)(2,1)S(1)} %activation.5.refs_0_.refs_1_), channel_id=1, source_target_pairs={{0,1},{1,0},{2,3},{3,2},{4,5},{5,4},{6,7},{7,6},{8,9},{9,8},{10,11... | collective-permute-start | bytes 589832 | tf_op jit(solution)/shard_map/ppermute | solution.py:40
  51.8 11.7 %collective-permute-start.12 = (bf16[32,1536]{1,0:T(8,128)(2,1)S(1)}, bf16[32,1536]{1,0:T(8,128)(2,1)S(1)}, u32[]{:S(2)}, u32[]{:S(2)}) collective-permute-start(bf16[32,1536]{1,0:T(8,128)(2,1)S(1)} %get-tuple-element.166), channel_id=1, source_target_pairs={{0,12},{4,0},{8,4},{12,8},{1,13},{5,1},{9,5},{13,9},{2,14},{6,2},{... | collective-permute-start | bytes 294920 | tf_op jit(solution)/shard_map/ppermute | solution.py:40
  53.8 10.4 %collective-permute-start.13 = (bf16[32,1536]{1,0:T(8,128)(2,1)S(1)}, bf16[32,1536]{1,0:T(8,128)(2,1)S(1)}, u32[]{:S(2)}, u32[]{:S(2)}) collective-permute-start(bf16[32,1536]{1,0:T(8,128)(2,1)S(1)} %get-tuple-element.167), channel_id=1, source_target_pairs={{0,8},{4,12},{8,0},{12,4},{1,9},{5,13},{9,1},{13,5},{2,10},{6,14},... | collective-permute-start | bytes 294920 | tf_op jit(solution)/shard_map/ppermute | solution.py:40
  54.7 9.4 %collective-permute-start.14 = (bf16[32,1536]{1,0:T(8,128)(2,1)S(1)}, bf16[32,1536]{1,0:T(8,128)(2,1)S(1)}, u32[]{:S(2)}, u32[]{:S(2)}) collective-permute-start(bf16[32,1536]{1,0:T(8,128)(2,1)S(1)} %get-tuple-element.168), channel_id=1, source_target_pairs={{0,4},{4,8},{8,12},{12,0},{1,5},{5,9},{9,13},{13,1},{2,6},{6,10},{... | collective-permute-start | bytes 294920 | tf_op jit(solution)/shard_map/ppermute | solution.py:40

commit v3 on v2

--- a/solution.py
+++ b/solution.py
@@ -9,7 +9,7 @@
 
 F32 = jnp.float32
 BF16 = jnp.bfloat16
-CHUNKS = ((4,), (4, 4), (4,))
+CHUNKS = ((8,), (4, 4))
 VMEM_SPEC = pl.BlockSpec(memory_space=pltpu.VMEM)
 SMEM_SPEC = pl.BlockSpec(memory_space=pltpu.SMEM)
 ANY_SPEC = pl.BlockSpec(memory_space=pl.ANY)

time: 65 us -> 63.9 us (0.983)
  waiting for transfers between devices: 3.41 us -> 5.41 us
  Pallas kernels: 44.9 us -> 43.3 us
  starting transfers between devices: 15.7 us -> 14.2 us
    ppermute x15 -> x12, waiting for transfers between devices: 3.41 us -> 5.41 us  [shift(): return lax.ppermute(x, axis, [(i, (i + by) % size) for i in range(size)])]
    ppermute x15 -> x12, starting transfers between devices: 15.7 us -> 14.2 us  [shift(): return lax.ppermute(x, axis, [(i, (i + by) % size) for i in range(size)])]
    pallas_call x6 -> x4, Pallas kernels: 11.9 us -> 10.8 us  [forward(): pl.pallas_call(functools.partial(forward_kernel, rows, pieces, ahead, out...]
    pallas_call x5 -> x4, Pallas kernels: 24.3 us -> 23.9 us  [backward(): pl.pallas_call(functools.partial(backward_kernel, where, rows, of or rang...]
  transfers between devices with their start and end apart: 15 -> 12, of which waited for: 5 -> 3; matrix products, arithmetic and copies ran while one was open for 0% -> 0% of each run, Pallas kernels for 57% -> 57%
where the time goes in v3:
time: 63.9 us; the launch traced here: 63.7 us
  Pallas kernels  43.3 us (68%)
  starting transfers between devices  14.2 us (22%)
  waiting for transfers between devices  5.41 us (8%)
  between operations  0.79 us (1%)
    pallas_call x4, Pallas kernels, backward(): pl.pallas_call(functools.partial(backward_kernel, where, rows, of or rang...  23.9 us
    ppermute x12, starting transfers between devices, shift(): return lax.ppermute(x, axis, [(i, (i + by) % size) for i in range(size)])  14.2 us
    pallas_call x4, Pallas kernels, forward(): pl.pallas_call(functools.partial(forward_kernel, rows, pieces, ahead, out...  10.8 us
    pallas_call x1, Pallas kernels, load(): pl.pallas_call(functools.partial(load_kernel, pieces), in_specs=[SMEM_SPE...  6.54 us
    ppermute x12, waiting for transfers between devices, shift(): return lax.ppermute(x, axis, [(i, (i + by) % size) for i in range(size)])  5.41 us
  transfers between devices with their start and end apart: 12, of which 3 were waited for; matrix products, arithmetic and copies ran while one was open for 0% of the time, Pallas kernels for 57%

profile of v3, /device:TPU:0, one launch (start us, length us, event | category | flops | bytes accessed | tf_op | source)
XLA Modules:
  0.0 63.7 jit_solution(12925900170044959210)
XLA Ops:
  0.6 0.8 %pack_rows.1.refs_0_ = bf16[32,1536]{1,0:T(8,128)(2,1)S(1)} custom-call(bf16[16,1536]{1,0:T(8,128)(2,1)} %tokens.1, bf16[16,1536]{1,0:T(8,128)(2,1)} %cot.1), custom_call_target="tpu_custom_call" | custom-call | bytes 196608 | tf_op jit(solution)/shard_map/pack_rows/pallas_call | solution.py:116
  1.5 5.1 %collective-permute-start.2 = (bf16[32,1536]{1,0:T(8,128)(2,1)S(1)}, bf16[32,1536]{1,0:T(8,128)(2,1)S(1)}, u32[]{:S(2)}, u32[]{:S(2)}) collective-permute-start(bf16[32,1536]{1,0:T(8,128)(2,1)S(1)} %pack_rows.1.refs_0_), channel_id=1, source_target_pairs={{0,12},{4,0},{8,4},{12,8},{1,13},{5,1},{9,5},{13,9},{2,14},{6,2},{... | collective-permute-start | bytes 294920 | tf_op jit(solution)/shard_map/ppermute | solution.py:40
  6.6 0.0 collective-permute-start.1
  6.6 1.0 %collective-permute-start = (bf16[32,1536]{1,0:T(8,128)(2,1)S(1)}, bf16[32,1536]{1,0:T(8,128)(2,1)S(1)}, u32[]{:S(2)}, u32[]{:S(2)}) collective-permute-start(bf16[32,1536]{1,0:T(8,128)(2,1)S(1)} %pack_rows.1.refs_0_), channel_id=1, source_target_pairs={{0,4},{4,8},{8,12},{12,0},{1,5},{5,9},{9,13},{13,1},{2,6},{6,10},{... | collective-permute-start | bytes 294920 | tf_op jit(solution)/shard_map/ppermute | solution.py:40
  7.6 6.5 %load_weights.1 = (bf16[1536,1024]{1,0:T(8,128)(2,1)S(1)}, bf16[1536,1024]{1,0:T(8,128)(2,1)S(1)}, bf16[1024,1536]{1,0:T(8,128)(2,1)S(1)}, bf16[1536,1024]{1,0:T...) custom-call(s32[1]{0:T(128)} %bitcast.me, bf16[1536,4096]{1,0:T(8,128)(2,1)} %refs_8_.3, ...), custom_call_target="tpu_custom_call" | custom-call | bytes 18874368 | tf_op jit(solution)/shard_map/load_weights/pallas_call | solution.py:90
  14.1 0.0 collective-permute-done.2.refs_3_
  14.2 1.2 %collective-permute-done.1.refs_2_ = bf16[32,1536]{1,0:T(8,128)(2,1)S(1)} collective-permute-done((bf16[32,1536]{1,0:T(8,128)(2,1)S(1)}, bf16[32,1536]{1,0:T(8,128)(2,1)S(1)}, u32[]{:S(2)}, u32[]{:S(2)}) %collective-permute-start.1) | collective-permute-done | bytes 98336 | tf_op jit(solution)/shard_map/ppermute | solution.py:40
  15.3 0.0 collective-permute-done.refs_1_
  15.3 2.4 %partial_sums.4 = (bf16[3,64,1024]{2,1,0:T(8,128)(2,1)S(1)}, bf16[64,1536]{1,0:T(8,128)(2,1)S(1)}, bf16[64,1536]{1,0:T(8,128)(2,1)S(1)}, bf16[1536,512]{1,0:T(8,...) custom-call(s32[1]{0:T(128)} %bitcast.me, bf16[32,1536]{1,0:T(8,128)(2,1)S(1)} %pack_rows.1.refs_0_, ...), custom_call_target="tpu_custom_call" | custom-call | flops 393216 | bytes 393216 | tf_op jit(solution)/shard_map/partial_sums/pallas_call | solution.py:177
  17.7 0.1 collective-permute-start.3
  17.8 2.4 %partial_sums.5 = (f32[3,64,1024]{2,1,0:T(8,128)S(1)}, bf16[1536,512]{1,0:T(8,128)(2,1)S(1)}, bf16[1536,512]{1,0:T(8,128)(2,1)S(1)}, bf16[512,1536]{1,0:T(8,128)(2,1)S(1)}) custom-call(s32[1]{0:T(128)} %bitcast.me, bf16[64,1536]{1,0:T(8,128)(2,1)S(1)} %get-tuple-element.106.refs_0_.refs_8_.refs_2_, ...), custom_call_target="tpu_custom_call" | custom-call | flops 393216 | bytes 393216 | tf_op jit(solution)/shard_map/partial_sums/pallas_call | solution.py:177
  20.2 0.0 collective-permute-done.3.received
  20.3 0.1 join_cores.2
  20.4 1.6 %collective-permute-start.6 = (bf16[3,64,1024]{2,1,0:T(8,128)(2,1)S(1)}, bf16[3,64,1024]{2,1,0:T(8,128)(2,1)S(1)}, u32[]{:S(2)}, u32[]{:S(2)}) collective-permute-start(bf16[3,64,1024]{2,1,0:T(8,128)(2,1)S(1)} %get-tuple-element.86), channel_id=1, source_target_pairs={{0,2},{2,0},{1,3},{3,1},{4,6},{6,4},{5,7},{7,5},{8,10},{10,8},{9,1... | collective-permute-start | bytes 1179656 | tf_op jit(solution)/shard_map/ppermute | solution.py:40
  21.9 3.8 %partial_sums.6 = (bf16[3,64,1024]{2,1,0:T(8,128)(2,1)S(1)}, bf16[1536,512]{1,0:T(8,128)(2,1)S(1)}, bf16[1536,512]{1,0:T(8,128)(2,1)S(1)}, bf16[512,1536]{1,0:T(...) custom-call(s32[1]{0:T(128)} %bitcast.me, ...), custom_call_target="tpu_custom_call" | custom-call | flops 393216 | bytes 393216 | tf_op jit(solution)/shard_map/partial_sums/pallas_call | solution.py:177
  25.8 0.3 collective-permute-start.4
  26.0 2.1 %partial_sums.7.mine = f32[3,64,1024]{2,1,0:T(8,128)S(1)} custom-call(s32[1]{0:T(128)} %bitcast.me, bf16[64,1536]{1,0:T(8,128)(2,1)S(1)} %get-tuple-element.106.refs_0_.refs_8_.refs_2_, bf16[64,1536]{1,0:T(8,128)(2,1)S(1)} %get-tuple-element.107.refs_1_.refs_9_.refs_3_, bf16[1536,512]{1,0:T(8,128)(2,1)S(1)} %get-tuple-element.95.refs_2_.refs_1_, ...), custom_call_target="tpu_custom_call" | custom-call | flops 393216 | bytes 393216 | tf_op jit(solution)/shard_map/partial_sums/pallas_call | solution.py:177
  28.2 3.8 %collective-permute-done.6.refs_1_ = bf16[3,64,1024]{2,1,0:T(8,128)(2,1)S(1)} collective-permute-done((bf16[3,64,1024]{2,1,0:T(8,128)(2,1)S(1)}, bf16[3,64,1024]{2,1,0:T(8,128)(2,1)S(1)}, u32[]{:S(2)}, u32[]{:S(2)}) %collective-permute-start.6) | collective-permute-done | bytes 393248 | tf_op jit(solution)/shard_map/ppermute | solution.py:40
  31.9 0.2 activation.2.refs_0_
  32.1 0.1 collective-permute-start.7
  32.2 0.0 collective-permute-done.4.received
  32.2 0.1 join_cores.3
  32.3 1.6 %collective-permute-start.5 = (bf16[3,64,1024]{2,1,0:T(8,128)(2,1)S(1)}, bf16[3,64,1024]{2,1,0:T(8,128)(2,1)S(1)}, u32[]{:S(2)}, u32[]{:S(2)}) collective-permute-start(bf16[3,64,1024]{2,1,0:T(8,128)(2,1)S(1)} %get-tuple-element.103), channel_id=1, source_target_pairs={{0,2},{2,0},{1,3},{3,1},{4,6},{6,4},{5,7},{7,5},{8,10},{10,8},{9,1... | collective-permute-start | bytes 1179656 | tf_op jit(solution)/shard_map/ppermute | solution.py:40
  33.9 0.0 collective-permute-done.7.refs_1_
  33.9 11.4 %backward.1 = (f32[64,1536]{1,0:T(8,128)S(1)}, f32[64,1536]{1,0:T(8,128)S(1)}, bf16[1536,4096]{1,0:T(8,128)(2,1)}, bf16[1536,4096]{1,0:T(8,128)(2,1)}, bf16[4096,1536]{1,0:T(8,128)(2,1)}) custom-call(s32[1]{0:T(128)} %bitcast.me, bf16[3,64,1024]{2,1,0:T(8,128)(2,1)S(1)} %activation.2.refs_0_, bf16[3,64,1024]{2,1,0:T(8,128)(2,1)S(1)} %collective-permute-done.7.refs_1_, ...), custom_call_target="tpu_custom_call" | custom-call | flops 2415919104 | bytes 37748736 | tf_op jit(solution)/shard_map/backward/pallas_call | solution.py:362
  45.3 0.0 collective-permute-done.5.refs_1_
  45.3 0.2 activation.3.refs_0_
  45.5 0.2 collective-permute-start.8
  45.8 2.5 %output_rows.2 = (f32[64,1536]{1,0:T(8,128)S(1)}, f32[64,1536]{1,0:T(8,128)S(1)}) custom-call(s32[1]{0:T(128)} %bitcast.me, bf16[3,64,1024]{2,1,0:T(8,128)(2,1)S(1)} %activation.3.refs_0_, bf16[1536,512]{1,0:T(8,128)(2,1)S(1)} %get-tuple-element.95.refs_2_.refs_1_, bf16[1536,512]{1,0:T(8,128)(2,1)S(1)} %get-tuple-element.96.refs_3_.refs_2_, ...), custom_call_target="tpu_custom_call" | custom-call | flops 603979776 | bytes 9437184 | tf_op jit(solution)/shard_map/output_rows/pallas_call | solution.py:362
  48.3 0.0 collective-permute-done.8.refs_0_.refs_1_
  48.3 2.5 %output_rows.3 = (f32[32,1536]{1,0:T(8,128)S(1)}, bf16[32,1536]{1,0:T(8,128)(2,1)S(1)}, bf16[32,1536]{1,0:T(8,128)(2,1)S(1)}, bf16[32,1536]{1,0:T(8,128)(2,1)S(1)}) custom-call(s32[1]{0:T(128)} %bitcast.me, bf16[3,64,1024]{2,1,0:T(8,128)(2,1)S(1)} %collective-permute-done.8.refs_0_.refs_1_, bf16[1536,512]{1,0:T(8,128)(2,1)S(1)} %get-tuple-element.89.refs_2_.refs_1_, ...), custom_call_target="tpu_custom_call" | custom-call | flops 603979776 | bytes 9437184 | tf_op jit(solution)/shard_map/output_rows/pallas_call | solution.py:362
  50.9 2.0 %collective-permute-start.9 = (bf16[32,1536]{1,0:T(8,128)(2,1)S(1)}, bf16[32,1536]{1,0:T(8,128)(2,1)S(1)}, u32[]{:S(2)}, u32[]{:S(2)}) collective-permute-start(bf16[32,1536]{1,0:T(8,128)(2,1)S(1)} %get-tuple-element.116), channel_id=1, source_target_pairs={{0,12},{4,0},{8,4},{12,8},{1,13},{5,1},{9,5},{13,9},{2,14},{6,2},{... | collective-permute-start | bytes 294920 | tf_op jit(solution)/shard_map/ppermute | solution.py:40
  52.9 0.8 %collective-permute-start.10 = (bf16[32,1536]{1,0:T(8,128)(2,1)S(1)}, bf16[32,1536]{1,0:T(8,128)(2,1)S(1)}, u32[]{:S(2)}, u32[]{:S(2)}) collective-permute-start(bf16[32,1536]{1,0:T(8,128)(2,1)S(1)} %get-tuple-element.117), channel_id=1, source_target_pairs={{0,8},{4,12},{8,0},{12,4},{1,9},{5,13},{9,1},{13,5},{2,10},{6,14},... | collective-permute-start | bytes 294920 | tf_op jit(solution)/shard_map/ppermute | solution.py:40
  53.7 1.5 %collective-permute-start.11 = (bf16[32,1536]{1,0:T(8,128)(2,1)S(1)}, bf16[32,1536]{1,0:T(8,128)(2,1)S(1)}, u32[]{:S(2)}, u32[]{:S(2)}) collective-permute-start(bf16[32,1536]{1,0:T(8,128)(2,1)S(1)} %get-tuple-element.118), channel_id=1, source_target_pairs={{0,4},{4,8},{8,12},{12,0},{1,5},{5,9},{9,13},{13,1},{2,6},{6,10},{... | collective-permute-start | bytes 294920 | tf_op jit(solution)/shard_map/ppermute | solution.py:40
  55.2 7.4 %weight_grads.1 = (bf16[1536,4096]{1,0:T(8,128)(2,1)}, bf16[1536,4096]{1,0:T(8,128)(2,1)}, bf16[4096,1536]{1,0:T(8,128)(2,1)}) custom-call(s32[1]{0:T(128)} %bitcast.me, bf16[3,64,1024]{2,1,0:T(8,128)(2,1)S(1)} %activation.3.refs_0_, ...), custom_call_target="tpu_custom_call", output_to_operand_aliasing={{0}: (5, {}), {1}: (6, {}), {2}: (7, {})} | custom-call | flops 1207959552 | bytes 18874368 | tf_op jit(solution)/shard_map/weight_grads/pallas_call | solution.py:362
  62.6 0.0 collective-permute-done.9.refs_1_
  62.6 0.4 collective-permute-done.10.refs_2_
  63.1 0.0 collective-permute-done.11.refs_3_
  63.1 0.7 %finish_rows.1 = (bf16[16,1536]{1,0:T(8,128)(2,1)}, bf16[16,1536]{1,0:T(8,128)(2,1)}) custom-call(f32[32,1536]{1,0:T(8,128)S(1)} %get-tuple-element.115.refs_0_, bf16[32,1536]{1,0:T(8,128)(2,1)S(1)} %collective-permute-done.9.refs_1_, bf16[32,1536]{1,0:T(8,128)(2,1)S(1)} %collective-permute-done.10.refs_2_, bf16[32,1536]{1,0:T(8,128)(2,1)S(1)} %collective-permute-done.11.refs_3_), custom_call_target="tpu_custom_call" | custom-call | tf_op jit(solution)/shard_map/finish_rows/pallas_call | solution.py:391
Async XLA Ops:
  1.5 12.7 %collective-permute-start.2 = (bf16[32,1536]{1,0:T(8,128)(2,1)S(1)}, bf16[32,1536]{1,0:T(8,128)(2,1)S(1)}, u32[]{:S(2)}, u32[]{:S(2)}) collective-permute-start(bf16[32,1536]{1,0:T(8,128)(2,1)S(1)} %pack_rows.1.refs_0_), channel_id=1, source_target_pairs={{0,12},{4,0},{8,4},{12,8},{1,13},{5,1},{9,5},{13,9},{2,14},{6,2},{... | collective-permute-start | bytes 294920 | tf_op jit(solution)/shard_map/ppermute | solution.py:40
  6.6 8.7 %collective-permute-start.1 = (bf16[32,1536]{1,0:T(8,128)(2,1)S(1)}, bf16[32,1536]{1,0:T(8,128)(2,1)S(1)}, u32[]{:S(2)}, u32[]{:S(2)}) collective-permute-start(bf16[32,1536]{1,0:T(8,128)(2,1)S(1)} %pack_rows.1.refs_0_), channel_id=1, source_target_pairs={{0,8},{4,12},{8,0},{12,4},{1,9},{5,13},{9,1},{13,5},{2,10},{6,14},... | collective-permute-start | bytes 294920 | tf_op jit(solution)/shard_map/ppermute | solution.py:40
  6.6 8.7 %collective-permute-start = (bf16[32,1536]{1,0:T(8,128)(2,1)S(1)}, bf16[32,1536]{1,0:T(8,128)(2,1)S(1)}, u32[]{:S(2)}, u32[]{:S(2)}) collective-permute-start(bf16[32,1536]{1,0:T(8,128)(2,1)S(1)} %pack_rows.1.refs_0_), channel_id=1, source_target_pairs={{0,4},{4,8},{8,12},{12,0},{1,5},{5,9},{9,13},{13,1},{2,6},{6,10},{... | collective-permute-start | bytes 294920 | tf_op jit(solution)/shard_map/ppermute | solution.py:40
  17.7 2.5 %collective-permute-start.3 = (bf16[3,64,1024]{2,1,0:T(8,128)(2,1)S(1)}, bf16[3,64,1024]{2,1,0:T(8,128)(2,1)S(1)}, u32[]{:S(2)}, u32[]{:S(2)}) collective-permute-start(bf16[3,64,1024]{2,1,0:T(8,128)(2,1)S(1)} %get-tuple-element.85), channel_id=1, source_target_pairs={{0,1},{1,0},{2,3},{3,2},{4,5},{5,4},{6,7},{7,6},{8,9},{9,8},{10,11... | collective-permute-start | bytes 1179656 | tf_op jit(solution)/shard_map/ppermute | solution.py:40
  20.4 11.6 %collective-permute-start.6 = (bf16[3,64,1024]{2,1,0:T(8,128)(2,1)S(1)}, bf16[3,64,1024]{2,1,0:T(8,128)(2,1)S(1)}, u32[]{:S(2)}, u32[]{:S(2)}) collective-permute-start(bf16[3,64,1024]{2,1,0:T(8,128)(2,1)S(1)} %get-tuple-element.86), channel_id=1, source_target_pairs={{0,2},{2,0},{1,3},{3,1},{4,6},{6,4},{5,7},{7,5},{8,10},{10,8},{9,1... | collective-permute-start | bytes 1179656 | tf_op jit(solution)/shard_map/ppermute | solution.py:40
  25.8 6.4 %collective-permute-start.4 = (bf16[3,64,1024]{2,1,0:T(8,128)(2,1)S(1)}, bf16[3,64,1024]{2,1,0:T(8,128)(2,1)S(1)}, u32[]{:S(2)}, u32[]{:S(2)}) collective-permute-start(bf16[3,64,1024]{2,1,0:T(8,128)(2,1)S(1)} %get-tuple-element.101), channel_id=1, source_target_pairs={{0,1},{1,0},{2,3},{3,2},{4,5},{5,4},{6,7},{7,6},{8,9},{9,8},{10,11... | collective-permute-start | bytes 1179656 | tf_op jit(solution)/shard_map/ppermute | solution.py:40
  32.1 1.8 %collective-permute-start.7 = (bf16[3,64,1024]{2,1,0:T(8,128)(2,1)S(1)}, bf16[3,64,1024]{2,1,0:T(8,128)(2,1)S(1)}, u32[]{:S(2)}, u32[]{:S(2)}) collective-permute-start(bf16[3,64,1024]{2,1,0:T(8,128)(2,1)S(1)} %activation.2.refs_0_), channel_id=1, source_target_pairs={{0,1},{1,0},{2,3},{3,2},{4,5},{5,4},{6,7},{7,6},{8,9},{9,8},{10,11... | collective-permute-start | bytes 1179656 | tf_op jit(solution)/shard_map/ppermute | solution.py:40
  32.3 13.0 %collective-permute-start.5 = (bf16[3,64,1024]{2,1,0:T(8,128)(2,1)S(1)}, bf16[3,64,1024]{2,1,0:T(8,128)(2,1)S(1)}, u32[]{:S(2)}, u32[]{:S(2)}) collective-permute-start(bf16[3,64,1024]{2,1,0:T(8,128)(2,1)S(1)} %get-tuple-element.103), channel_id=1, source_target_pairs={{0,2},{2,0},{1,3},{3,1},{4,6},{6,4},{5,7},{7,5},{8,10},{10,8},{9,1... | collective-permute-start | bytes 1179656 | tf_op jit(solution)/shard_map/ppermute | solution.py:40
  45.5 2.8 %collective-permute-start.8 = (bf16[3,64,1024]{2,1,0:T(8,128)(2,1)S(1)}, bf16[3,64,1024]{2,1,0:T(8,128)(2,1)S(1)}, u32[]{:S(2)}, u32[]{:S(2)}) collective-permute-start(bf16[3,64,1024]{2,1,0:T(8,128)(2,1)S(1)} %activation.3.refs_0_), channel_id=1, source_target_pairs={{0,1},{1,0},{2,3},{3,2},{4,5},{5,4},{6,7},{7,6},{8,9},{9,8},{10,11... | collective-permute-start | bytes 1179656 | tf_op jit(solution)/shard_map/ppermute | solution.py:40
  50.9 11.8 %collective-permute-start.9 = (bf16[32,1536]{1,0:T(8,128)(2,1)S(1)}, bf16[32,1536]{1,0:T(8,128)(2,1)S(1)}, u32[]{:S(2)}, u32[]{:S(2)}) collective-permute-start(bf16[32,1536]{1,0:T(8,128)(2,1)S(1)} %get-tuple-element.116), channel_id=1, source_target_pairs={{0,12},{4,0},{8,4},{12,8},{1,13},{5,1},{9,5},{13,9},{2,14},{6,2},{... | collective-permute-start | bytes 294920 | tf_op jit(solution)/shard_map/ppermute | solution.py:40
  52.9 10.2 %collective-permute-start.10 = (bf16[32,1536]{1,0:T(8,128)(2,1)S(1)}, bf16[32,1536]{1,0:T(8,128)(2,1)S(1)}, u32[]{:S(2)}, u32[]{:S(2)}) collective-permute-start(bf16[32,1536]{1,0:T(8,128)(2,1)S(1)} %get-tuple-element.117), channel_id=1, source_target_pairs={{0,8},{4,12},{8,0},{12,4},{1,9},{5,13},{9,1},{13,5},{2,10},{6,14},... | collective-permute-start | bytes 294920 | tf_op jit(solution)/shard_map/ppermute | solution.py:40
  53.7 9.3 %collective-permute-start.11 = (bf16[32,1536]{1,0:T(8,128)(2,1)S(1)}, bf16[32,1536]{1,0:T(8,128)(2,1)S(1)}, u32[]{:S(2)}, u32[]{:S(2)}) collective-permute-start(bf16[32,1536]{1,0:T(8,128)(2,1)S(1)} %get-tuple-element.118), channel_id=1, source_target_pairs={{0,4},{4,8},{8,12},{12,0},{1,5},{5,9},{9,13},{13,1},{2,6},{6,10},{... | collective-permute-start | bytes 294920 | tf_op jit(solution)/shard_map/ppermute | solution.py:40

commit v4 on v3

--- a/solution.py
+++ b/solution.py
@@ -9,7 +9,7 @@
 
 F32 = jnp.float32
 BF16 = jnp.bfloat16
-CHUNKS = ((8,), (4, 4))
+CHUNKS = ((4, 4), (4, 4))
 VMEM_SPEC = pl.BlockSpec(memory_space=pltpu.VMEM)
 SMEM_SPEC = pl.BlockSpec(memory_space=pltpu.SMEM)
 ANY_SPEC = pl.BlockSpec(memory_space=pl.ANY)
@@ -192,22 +192,30 @@
     return out[0], out[1:3] if assemble else acts, loaded
 
 
-def join_kernel(mine, received, kept, sent):
-    total = mine[...] + received[...].astype(F32)
-    kept[...] = total
-    sent[...] = total.astype(BF16)
-
-
-def join(mine, received):
-    return pl.pallas_call(
+def join_kernel(mine, received, *outs):
+    first = 0
+    for kept, sent in zip(outs[0::2], outs[1::2]):
+        here = slice(first, first + kept.shape[2])
+        first += kept.shape[2]
+        total = mine[:, :, here] + received[:, :, here].astype(F32)
+        kept[...] = total
+        sent[...] = total.astype(BF16)
+
+
+def join(mine, received, widths):
+    outs = []
+    for width in widths:
+        outs += [in_vmem((*mine.shape[:2], width), dtype) for dtype in (F32, BF16)]
+    out = pl.pallas_call(
         join_kernel,
         in_specs=[VMEM_SPEC] * 2,
-        out_specs=[VMEM_SPEC] * 2,
-        out_shape=[in_vmem(mine.shape, F32), in_vmem(mine.shape, BF16)],
+        out_specs=[VMEM_SPEC] * len(outs),
+        out_shape=outs,
         compiler_params=params(),
         cost_estimate=cost(mine.size, 12 * mine.size),
         name="join_cores",
     )(mine, received)
+    return list(zip(out[0::2], out[1::2]))
 
 
 def activate_kernel(*refs):
@@ -442,7 +450,7 @@
             plan[-1].append(queue.pop(0))
     held = dict(zip(plan[0], load(me, plan[0], whole)))
     acts, held = tied(acts, held)
-    kept, products, crossed = [], [], []
+    kept, products, crossed, steps = [], [], [], []
     step = 1
     for mine, other in parts:
         made = []
@@ -455,25 +463,29 @@
             step += 1
             made.append(out)
         products.append(made)
-        total, out = join(made[1], shift(made[0], "inner", inner, 1))
-        acts, _ = lax.optimization_barrier((acts, out))
-        kept.append(total)
-        crossed.append([shift(out, "narrow", narrow, k) for k in range(1, narrow)])
+        if mine is parts[0][0]:
+            spans = [([m], [o]) for m, o in zip(mine, other)]
+        else:
+            spans = [(mine, other)]
+        widths = [sum(p[-1] for p in span[0]) for span in spans]
+        joined = join(made[1], shift(made[0], "inner", inner, 1), widths)
+        acts, _ = lax.optimization_barrier((acts, joined[-1][1]))
+        for span, (total, out) in zip(spans, joined):
+            steps.append(span)
+            kept.append(total)
+            crossed.append([shift(out, "narrow", narrow, k) for k in range(1, narrow)])
     tokens_all, cot_all = acts
     crossed[0], _ = lax.optimization_barrier((crossed[0], products[-1]))
     sums, grads, later = (), (), []
-    for i, where in enumerate(parts):
+    for i, where in enumerate(steps):
         own = activate(kept[i], crossed[i])
         acts = [own, shift(own, "inner", inner, 1)]
         weights = [[held[piece] for piece in pieces] for pieces in where]
-        if where is parts[-1]:
+        if i == len(steps) - 1:
             later += list(zip(where, acts))
         else:
-            of = (0, 1)
-            if i == len(parts) - 2 and i:
-                of, later = (0,), [(where[1], acts[1])]
             sums, grads = backward(
-                me, where, acts, weights, tokens_all, cot_all, sums, grads, hidden, of=of
+                me, where, acts, weights, tokens_all, cot_all, sums, grads, hidden
             )
             crossed[i + 1], sums = lax.optimization_barrier((crossed[i + 1], sums))
     for last, (pieces, act, three) in enumerate(zip(where, acts, weights)):

time: 63.9 us -> 63.8 us (level)
  waiting for transfers between devices: 5.41 us -> 3.07 us
  Pallas kernels: 43.3 us -> 44.7 us
  starting transfers between devices: 14.2 us -> 15.1 us
    ppermute x12 -> x14, waiting for transfers between devices: 5.41 us -> 3.07 us  [shift(): return lax.ppermute(x, axis, [(i, (i + by) % size) for i in range(size)])]
    pallas_call x4 -> x5, Pallas kernels: 23.9 us -> 25.1 us  [backward(): pl.pallas_call(functools.partial(backward_kernel, where, rows, of or rang...]
    ppermute x12 -> x14, starting transfers between devices: 14.2 us -> 15.1 us  [shift(): return lax.ppermute(x, axis, [(i, (i + by) % size) for i in range(size)])]
  transfers between devices with their start and end apart: 12 -> 14, of which waited for: 3 -> 3; matrix products, arithmetic and copies ran while one was open for 0% -> 0% of each run, Pallas kernels for 57% -> 59%
where the time goes in v4:
time: 63.8 us; the launch traced here: 63.7 us
  Pallas kernels  44.7 us (70%)
  starting transfers between devices  15.1 us (24%)
  waiting for transfers between devices  3.07 us (5%)
  between operations  0.82 us (1%)
    pallas_call x5, Pallas kernels, backward(): pl.pallas_call(functools.partial(backward_kernel, where, rows, of or rang...  25.1 us
    ppermute x14, starting transfers between devices, shift(): return lax.ppermute(x, axis, [(i, (i + by) % size) for i in range(size)])  15.1 us
    pallas_call x4, Pallas kernels, forward(): pl.pallas_call(functools.partial(forward_kernel, rows, pieces, ahead, out...  10.8 us
    pallas_call x1, Pallas kernels, load(): pl.pallas_call(functools.partial(load_kernel, pieces), in_specs=[SMEM_SPE...  6.62 us
    ppermute x14, waiting for transfers between devices, shift(): return lax.ppermute(x, axis, [(i, (i + by) % size) for i in range(size)])  3.07 us
  transfers between devices with their start and end apart: 14, of which 3 were waited for; matrix products, arithmetic and copies ran while one was open for 0% of the time, Pallas kernels for 59%

profile of v4, /device:TPU:0, one launch (start us, length us, event | category | flops | bytes accessed | tf_op | source)
XLA Modules:
  0.0 63.7 jit_solution(8724610571950375768)
XLA Ops:
  0.6 0.8 %pack_rows.1.refs_0_ = bf16[32,1536]{1,0:T(8,128)(2,1)S(1)} custom-call(bf16[16,1536]{1,0:T(8,128)(2,1)} %tokens.1, bf16[16,1536]{1,0:T(8,128)(2,1)} %cot.1), custom_call_target="tpu_custom_call" | custom-call | bytes 196608 | tf_op jit(solution)/shard_map/pack_rows/pallas_call | solution.py:116
  1.5 5.1 %collective-permute-start.2 = (bf16[32,1536]{1,0:T(8,128)(2,1)S(1)}, bf16[32,1536]{1,0:T(8,128)(2,1)S(1)}, u32[]{:S(2)}, u32[]{:S(2)}) collective-permute-start(bf16[32,1536]{1,0:T(8,128)(2,1)S(1)} %pack_rows.1.refs_0_), channel_id=1, source_target_pairs={{0,12},{4,0},{8,4},{12,8},{1,13},{5,1},{9,5},{13,9},{2,14},{6,2},{... | collective-permute-start | bytes 294920 | tf_op jit(solution)/shard_map/ppermute | solution.py:40
  6.6 0.0 collective-permute-start.1
  6.6 1.0 %collective-permute-start = (bf16[32,1536]{1,0:T(8,128)(2,1)S(1)}, bf16[32,1536]{1,0:T(8,128)(2,1)S(1)}, u32[]{:S(2)}, u32[]{:S(2)}) collective-permute-start(bf16[32,1536]{1,0:T(8,128)(2,1)S(1)} %pack_rows.1.refs_0_), channel_id=1, source_target_pairs={{0,4},{4,8},{8,12},{12,0},{1,5},{5,9},{9,13},{13,1},{2,6},{6,10},{... | collective-permute-start | bytes 294920 | tf_op jit(solution)/shard_map/ppermute | solution.py:40
  7.6 6.6 %load_weights.1 = (bf16[1536,512]{1,0:T(8,128)(2,1)S(1)}, bf16[1536,512]{1,0:T(8,128)(2,1)S(1)}, bf16[512,1536]{1,0:T(8,128)(2,1)S(1)}, bf16[1536,512]{1,0:T(8,1...) custom-call(s32[1]{0:T(128)} %bitcast.me, ...), custom_call_target="tpu_custom_call" | custom-call | bytes 18874368 | tf_op jit(solution)/shard_map/load_weights/pallas_call | solution.py:90
  14.2 0.0 collective-permute-done.2.refs_3_
  14.2 1.1 %collective-permute-done.1.refs_2_ = bf16[32,1536]{1,0:T(8,128)(2,1)S(1)} collective-permute-done((bf16[32,1536]{1,0:T(8,128)(2,1)S(1)}, bf16[32,1536]{1,0:T(8,128)(2,1)S(1)}, u32[]{:S(2)}, u32[]{:S(2)}) %collective-permute-start.1) | collective-permute-done | bytes 98336 | tf_op jit(solution)/shard_map/ppermute | solution.py:40
  15.3 0.0 collective-permute-done.refs_1_
  15.3 2.4 %partial_sums.4 = (bf16[3,64,1024]{2,1,0:T(8,128)(2,1)S(1)}, bf16[64,1536]{1,0:T(8,128)(2,1)S(1)}, bf16[64,1536]{1,0:T(8,128)(2,1)S(1)}, bf16[1536,512]{1,0:T(8,...) custom-call(s32[1]{0:T(128)} %bitcast.me, bf16[32,1536]{1,0:T(8,128)(2,1)S(1)} %pack_rows.1.refs_0_, ...), custom_call_target="tpu_custom_call" | custom-call | flops 393216 | bytes 393216 | tf_op jit(solution)/shard_map/partial_sums/pallas_call | solution.py:177
  17.7 0.1 collective-permute-start.3
  17.8 2.4 %partial_sums.5 = (f32[3,64,1024]{2,1,0:T(8,128)S(1)}, bf16[1536,512]{1,0:T(8,128)(2,1)S(1)}, bf16[1536,512]{1,0:T(8,128)(2,1)S(1)}, bf16[512,1536]{1,0:T(8,128)(2,1)S(1)}) custom-call(s32[1]{0:T(128)} %bitcast.me, bf16[64,1536]{1,0:T(8,128)(2,1)S(1)} %get-tuple-element.142.refs_0_.refs_8_.refs_2_, ...), custom_call_target="tpu_custom_call" | custom-call | flops 393216 | bytes 393216 | tf_op jit(solution)/shard_map/partial_sums/pallas_call | solution.py:177
  20.3 0.0 collective-permute-done.3.received
  20.3 0.1 join_cores.2
  20.4 1.6 %collective-permute-start.7 = (bf16[3,64,512]{2,1,0:T(8,128)(2,1)S(1)}, bf16[3,64,512]{2,1,0:T(8,128)(2,1)S(1)}, u32[]{:S(2)}, u32[]{:S(2)}) collective-permute-start(bf16[3,64,512]{2,1,0:T(8,128)(2,1)S(1)} %get-tuple-element.140), channel_id=1, source_target_pairs={{0,2},{2,0},{1,3},{3,1},{4,6},{6,4},{5,7},{7,5},{8,10},{10,8},{9,1... | collective-permute-start | bytes 589832 | tf_op jit(solution)/shard_map/ppermute | solution.py:40
  21.9 3.8 %partial_sums.6 = (bf16[3,64,1024]{2,1,0:T(8,128)(2,1)S(1)}, bf16[1536,512]{1,0:T(8,128)(2,1)S(1)}, bf16[1536,512]{1,0:T(8,128)(2,1)S(1)}, bf16[512,1536]{1,0:T(...) custom-call(s32[1]{0:T(128)} %bitcast.me, ...), custom_call_target="tpu_custom_call" | custom-call | flops 393216 | bytes 393216 | tf_op jit(solution)/shard_map/partial_sums/pallas_call | solution.py:177
  25.8 0.3 collective-permute-start.4
  26.1 2.1 %partial_sums.7.mine = f32[3,64,1024]{2,1,0:T(8,128)S(1)} custom-call(s32[1]{0:T(128)} %bitcast.me, bf16[64,1536]{1,0:T(8,128)(2,1)S(1)} %get-tuple-element.142.refs_0_.refs_8_.refs_2_, bf16[64,1536]{1,0:T(8,128)(2,1)S(1)} %get-tuple-element.143.refs_1_.refs_9_.refs_3_, bf16[1536,512]{1,0:T(8,128)(2,1)S(1)} %get-tuple-element.129.refs_2_.refs_1_, ...), custom_call_target="tpu_custom_call" | custom-call | flops 393216 | bytes 393216 | tf_op jit(solution)/shard_map/partial_sums/pallas_call | solution.py:177
  28.2 0.0 collective-permute-done.7.refs_1_
  28.2 0.1 activation.3.refs_0_
  28.3 0.4 collective-permute-start.8
  28.7 0.8 %collective-permute-start.6 = (bf16[3,64,512]{2,1,0:T(8,128)(2,1)S(1)}, bf16[3,64,512]{2,1,0:T(8,128)(2,1)S(1)}, u32[]{:S(2)}, u32[]{:S(2)}) collective-permute-start(bf16[3,64,512]{2,1,0:T(8,128)(2,1)S(1)} %get-tuple-element.120), channel_id=1, source_target_pairs={{0,2},{2,0},{1,3},{3,1},{4,6},{6,4},{5,7},{7,5},{8,10},{10,8},{9,1... | collective-permute-start | bytes 589832 | tf_op jit(solution)/shard_map/ppermute | solution.py:40
  29.5 0.0 collective-permute-done.4.received
  29.5 0.1 join_cores.3
  29.6 1.3 %collective-permute-start.5 = (bf16[3,64,1024]{2,1,0:T(8,128)(2,1)S(1)}, bf16[3,64,1024]{2,1,0:T(8,128)(2,1)S(1)}, u32[]{:S(2)}, u32[]{:S(2)}) collective-permute-start(bf16[3,64,1024]{2,1,0:T(8,128)(2,1)S(1)} %get-tuple-element.137), channel_id=1, source_target_pairs={{0,2},{2,0},{1,3},{3,1},{4,6},{6,4},{5,7},{7,5},{8,10},{10,8},{9,1... | collective-permute-start | bytes 1179656 | tf_op jit(solution)/shard_map/ppermute | solution.py:40
  30.9 0.0 collective-permute-done.8.refs_1_
  30.9 6.2 %backward.2 = (f32[64,1536]{1,0:T(8,128)S(1)}, f32[64,1536]{1,0:T(8,128)S(1)}, bf16[1536,4096]{1,0:T(8,128)(2,1)}, bf16[1536,4096]{1,0:T(8,128)(2,1)}, bf16[4096,1536]{1,0:T(8,128)(2,1)}) custom-call(s32[1]{0:T(128)} %bitcast.me, bf16[3,64,512]{2,1,0:T(8,128)(2,1)S(1)} %activation.3.refs_0_, bf16[3,64,512]{2,1,0:T(8,128)(2,1)S(1)} %collective-permute-done.8.refs_1_, ...), custom_call_target="tpu_custom_call" | custom-call | flops 1207959552 | bytes 18874368 | tf_op jit(solution)/shard_map/backward/pallas_call | solution.py:370
  37.1 0.0 collective-permute-done.6.refs_1_
  37.1 0.1 activation.4.refs_0_
  37.2 0.1 collective-permute-start.9
  37.3 1.4 %collective-permute-done.9.refs_1_ = bf16[3,64,512]{2,1,0:T(8,128)(2,1)S(1)} collective-permute-done((bf16[3,64,512]{2,1,0:T(8,128)(2,1)S(1)}, bf16[3,64,512]{2,1,0:T(8,128)(2,1)S(1)}, u32[]{:S(2)}, u32[]{:S(2)}) %collective-permute-start.9) | collective-permute-done | bytes 196640 | tf_op jit(solution)/shard_map/ppermute | solution.py:40
  38.7 6.5 %backward.3 = (f32[64,1536]{1,0:T(8,128)S(1)}, f32[64,1536]{1,0:T(8,128)S(1)}, bf16[1536,4096]{1,0:T(8,128)(2,1)}, bf16[1536,4096]{1,0:T(8,128)(2,1)}, bf16[4096,1536]{1,0:T(8,128)(2,1)}) custom-call(s32[1]{0:T(128)} %bitcast.me, bf16[3,64,512]{2,1,0:T(8,128)(2,1)S(1)} %activation.4.refs_0_, ...), custom_call_target="tpu_custom_call", output_to_operand_aliasing={{2}: (13, {}), {3}: (14, {}), {4}: (15, {})} | custom-call | flops 1207959552 | bytes 18874368 | tf_op jit(solution)/shard_map/backward/pallas_call | solution.py:370
  45.2 0.0 collective-permute-done.5.refs_1_
  45.2 0.2 activation.5.refs_0_
  45.4 0.2 collective-permute-start.10
  45.6 2.6 %output_rows.2 = (f32[64,1536]{1,0:T(8,128)S(1)}, f32[64,1536]{1,0:T(8,128)S(1)}) custom-call(s32[1]{0:T(128)} %bitcast.me, bf16[3,64,1024]{2,1,0:T(8,128)(2,1)S(1)} %activation.5.refs_0_, bf16[1536,512]{1,0:T(8,128)(2,1)S(1)} %get-tuple-element.129.refs_2_.refs_1_, bf16[1536,512]{1,0:T(8,128)(2,1)S(1)} %get-tuple-element.130.refs_3_.refs_2_, ...), custom_call_target="tpu_custom_call" | custom-call | flops 603979776 | bytes 9437184 | tf_op jit(solution)/shard_map/output_rows/pallas_call | solution.py:370
  48.1 0.0 collective-permute-done.10.refs_0_.refs_1_
  48.1 2.5 %output_rows.3 = (f32[32,1536]{1,0:T(8,128)S(1)}, bf16[32,1536]{1,0:T(8,128)(2,1)S(1)}, bf16[32,1536]{1,0:T(8,128)(2,1)S(1)}, bf16[32,1536]{1,0:T(8,128)(2,1)S(1)}) custom-call(s32[1]{0:T(128)} %bitcast.me, bf16[3,64,1024]{2,1,0:T(8,128)(2,1)S(1)} %collective-permute-done.10.refs_0_.refs_1_, bf16[1536,512]{1,0:T(8,128)(2,1)S(1)} %get-tuple-element.123.refs_2_.refs_1_, ...), custom_call_target="tpu_custom_call" | custom-call | flops 603979776 | bytes 9437184 | tf_op jit(solution)/shard_map/output_rows/pallas_call | solution.py:370
  50.7 2.0 %collective-permute-start.11 = (bf16[32,1536]{1,0:T(8,128)(2,1)S(1)}, bf16[32,1536]{1,0:T(8,128)(2,1)S(1)}, u32[]{:S(2)}, u32[]{:S(2)}) collective-permute-start(bf16[32,1536]{1,0:T(8,128)(2,1)S(1)} %get-tuple-element.160), channel_id=1, source_target_pairs={{0,12},{4,0},{8,4},{12,8},{1,13},{5,1},{9,5},{13,9},{2,14},{6,2},{... | collective-permute-start | bytes 294920 | tf_op jit(solution)/shard_map/ppermute | solution.py:40
  52.7 0.9 %collective-permute-start.12 = (bf16[32,1536]{1,0:T(8,128)(2,1)S(1)}, bf16[32,1536]{1,0:T(8,128)(2,1)S(1)}, u32[]{:S(2)}, u32[]{:S(2)}) collective-permute-start(bf16[32,1536]{1,0:T(8,128)(2,1)S(1)} %get-tuple-element.161), channel_id=1, source_target_pairs={{0,8},{4,12},{8,0},{12,4},{1,9},{5,13},{9,1},{13,5},{2,10},{6,14},... | collective-permute-start | bytes 294920 | tf_op jit(solution)/shard_map/ppermute | solution.py:40
  53.6 1.4 %collective-permute-start.13 = (bf16[32,1536]{1,0:T(8,128)(2,1)S(1)}, bf16[32,1536]{1,0:T(8,128)(2,1)S(1)}, u32[]{:S(2)}, u32[]{:S(2)}) collective-permute-start(bf16[32,1536]{1,0:T(8,128)(2,1)S(1)} %get-tuple-element.162), channel_id=1, source_target_pairs={{0,4},{4,8},{8,12},{12,0},{1,5},{5,9},{9,13},{13,1},{2,6},{6,10},{... | collective-permute-start | bytes 294920 | tf_op jit(solution)/shard_map/ppermute | solution.py:40
  55.0 7.4 %weight_grads.1 = (bf16[1536,4096]{1,0:T(8,128)(2,1)}, bf16[1536,4096]{1,0:T(8,128)(2,1)}, bf16[4096,1536]{1,0:T(8,128)(2,1)}) custom-call(s32[1]{0:T(128)} %bitcast.me, bf16[3,64,1024]{2,1,0:T(8,128)(2,1)S(1)} %activation.5.refs_0_, ...), custom_call_target="tpu_custom_call", output_to_operand_aliasing={{0}: (5, {}), {1}: (6, {}), {2}: (7, {})} | custom-call | flops 1207959552 | bytes 18874368 | tf_op jit(solution)/shard_map/weight_grads/pallas_call | solution.py:370
  62.5 0.0 collective-permute-done.11.refs_1_
  62.5 0.5 collective-permute-done.12.refs_2_
  63.0 0.0 collective-permute-done.13.refs_3_
  63.0 0.7 %finish_rows.1 = (bf16[16,1536]{1,0:T(8,128)(2,1)}, bf16[16,1536]{1,0:T(8,128)(2,1)}) custom-call(f32[32,1536]{1,0:T(8,128)S(1)} %get-tuple-element.159.refs_0_, bf16[32,1536]{1,0:T(8,128)(2,1)S(1)} %collective-permute-done.11.refs_1_, bf16[32,1536]{1,0:T(8,128)(2,1)S(1)} %collective-permute-done.12.refs_2_, bf16[32,1536]{1,0:T(8,128)(2,1)S(1)} %collective-permute-done.13.refs_3_), custom_call_target="tpu_custom_call" | custom-call | tf_op jit(solution)/shard_map/finish_rows/pallas_call | solution.py:399
Async XLA Ops:
  1.5 12.8 %collective-permute-start.2 = (bf16[32,1536]{1,0:T(8,128)(2,1)S(1)}, bf16[32,1536]{1,0:T(8,128)(2,1)S(1)}, u32[]{:S(2)}, u32[]{:S(2)}) collective-permute-start(bf16[32,1536]{1,0:T(8,128)(2,1)S(1)} %pack_rows.1.refs_0_), channel_id=1, source_target_pairs={{0,12},{4,0},{8,4},{12,8},{1,13},{5,1},{9,5},{13,9},{2,14},{6,2},{... | collective-permute-start | bytes 294920 | tf_op jit(solution)/shard_map/ppermute | solution.py:40
  6.6 8.7 %collective-permute-start.1 = (bf16[32,1536]{1,0:T(8,128)(2,1)S(1)}, bf16[32,1536]{1,0:T(8,128)(2,1)S(1)}, u32[]{:S(2)}, u32[]{:S(2)}) collective-permute-start(bf16[32,1536]{1,0:T(8,128)(2,1)S(1)} %pack_rows.1.refs_0_), channel_id=1, source_target_pairs={{0,8},{4,12},{8,0},{12,4},{1,9},{5,13},{9,1},{13,5},{2,10},{6,14},... | collective-permute-start | bytes 294920 | tf_op jit(solution)/shard_map/ppermute | solution.py:40
  6.6 8.7 %collective-permute-start = (bf16[32,1536]{1,0:T(8,128)(2,1)S(1)}, bf16[32,1536]{1,0:T(8,128)(2,1)S(1)}, u32[]{:S(2)}, u32[]{:S(2)}) collective-permute-start(bf16[32,1536]{1,0:T(8,128)(2,1)S(1)} %pack_rows.1.refs_0_), channel_id=1, source_target_pairs={{0,4},{4,8},{8,12},{12,0},{1,5},{5,9},{9,13},{13,1},{2,6},{6,10},{... | collective-permute-start | bytes 294920 | tf_op jit(solution)/shard_map/ppermute | solution.py:40
  17.7 2.5 %collective-permute-start.3 = (bf16[3,64,1024]{2,1,0:T(8,128)(2,1)S(1)}, bf16[3,64,1024]{2,1,0:T(8,128)(2,1)S(1)}, u32[]{:S(2)}, u32[]{:S(2)}) collective-permute-start(bf16[3,64,1024]{2,1,0:T(8,128)(2,1)S(1)} %get-tuple-element.119), channel_id=1, source_target_pairs={{0,1},{1,0},{2,3},{3,2},{4,5},{5,4},{6,7},{7,6},{8,9},{9,8},{10,11... | collective-permute-start | bytes 1179656 | tf_op jit(solution)/shard_map/ppermute | solution.py:40
  20.4 7.8 %collective-permute-start.7 = (bf16[3,64,512]{2,1,0:T(8,128)(2,1)S(1)}, bf16[3,64,512]{2,1,0:T(8,128)(2,1)S(1)}, u32[]{:S(2)}, u32[]{:S(2)}) collective-permute-start(bf16[3,64,512]{2,1,0:T(8,128)(2,1)S(1)} %get-tuple-element.140), channel_id=1, source_target_pairs={{0,2},{2,0},{1,3},{3,1},{4,6},{6,4},{5,7},{7,5},{8,10},{10,8},{9,1... | collective-permute-start | bytes 589832 | tf_op jit(solution)/shard_map/ppermute | solution.py:40
  25.8 3.7 %collective-permute-start.4 = (bf16[3,64,1024]{2,1,0:T(8,128)(2,1)S(1)}, bf16[3,64,1024]{2,1,0:T(8,128)(2,1)S(1)}, u32[]{:S(2)}, u32[]{:S(2)}) collective-permute-start(bf16[3,64,1024]{2,1,0:T(8,128)(2,1)S(1)} %get-tuple-element.135), channel_id=1, source_target_pairs={{0,1},{1,0},{2,3},{3,2},{4,5},{5,4},{6,7},{7,6},{8,9},{9,8},{10,11... | collective-permute-start | bytes 1179656 | tf_op jit(solution)/shard_map/ppermute | solution.py:40
  28.3 2.6 %collective-permute-start.8 = (bf16[3,64,512]{2,1,0:T(8,128)(2,1)S(1)}, bf16[3,64,512]{2,1,0:T(8,128)(2,1)S(1)}, u32[]{:S(2)}, u32[]{:S(2)}) collective-permute-start(bf16[3,64,512]{2,1,0:T(8,128)(2,1)S(1)} %activation.3.refs_0_), channel_id=1, source_target_pairs={{0,1},{1,0},{2,3},{3,2},{4,5},{5,4},{6,7},{7,6},{8,9},{9,8},{10,11... | collective-permute-start | bytes 589832 | tf_op jit(solution)/shard_map/ppermute | solution.py:40
  28.7 8.4 %collective-permute-start.6 = (bf16[3,64,512]{2,1,0:T(8,128)(2,1)S(1)}, bf16[3,64,512]{2,1,0:T(8,128)(2,1)S(1)}, u32[]{:S(2)}, u32[]{:S(2)}) collective-permute-start(bf16[3,64,512]{2,1,0:T(8,128)(2,1)S(1)} %get-tuple-element.120), channel_id=1, source_target_pairs={{0,2},{2,0},{1,3},{3,1},{4,6},{6,4},{5,7},{7,5},{8,10},{10,8},{9,1... | collective-permute-start | bytes 589832 | tf_op jit(solution)/shard_map/ppermute | solution.py:40
  29.6 15.6 %collective-permute-start.5 = (bf16[3,64,1024]{2,1,0:T(8,128)(2,1)S(1)}, bf16[3,64,1024]{2,1,0:T(8,128)(2,1)S(1)}, u32[]{:S(2)}, u32[]{:S(2)}) collective-permute-start(bf16[3,64,1024]{2,1,0:T(8,128)(2,1)S(1)} %get-tuple-element.137), channel_id=1, source_target_pairs={{0,2},{2,0},{1,3},{3,1},{4,6},{6,4},{5,7},{7,5},{8,10},{10,8},{9,1... | collective-permute-start | bytes 1179656 | tf_op jit(solution)/shard_map/ppermute | solution.py:40
  37.2 1.5 %collective-permute-start.9 = (bf16[3,64,512]{2,1,0:T(8,128)(2,1)S(1)}, bf16[3,64,512]{2,1,0:T(8,128)(2,1)S(1)}, u32[]{:S(2)}, u32[]{:S(2)}) collective-permute-start(bf16[3,64,512]{2,1,0:T(8,128)(2,1)S(1)} %activation.4.refs_0_), channel_id=1, source_target_pairs={{0,1},{1,0},{2,3},{3,2},{4,5},{5,4},{6,7},{7,6},{8,9},{9,8},{10,11... | collective-permute-start | bytes 589832 | tf_op jit(solution)/shard_map/ppermute | solution.py:40
  45.4 2.8 %collective-permute-start.10 = (bf16[3,64,1024]{2,1,0:T(8,128)(2,1)S(1)}, bf16[3,64,1024]{2,1,0:T(8,128)(2,1)S(1)}, u32[]{:S(2)}, u32[]{:S(2)}) collective-permute-start(bf16[3,64,1024]{2,1,0:T(8,128)(2,1)S(1)} %activation.5.refs_0_), channel_id=1, source_target_pairs={{0,1},{1,0},{2,3},{3,2},{4,5},{5,4},{6,7},{7,6},{8,9},{9,8},{10,11... | collective-permute-start | bytes 1179656 | tf_op jit(solution)/shard_map/ppermute | solution.py:40
  50.7 11.8 %collective-permute-start.11 = (bf16[32,1536]{1,0:T(8,128)(2,1)S(1)}, bf16[32,1536]{1,0:T(8,128)(2,1)S(1)}, u32[]{:S(2)}, u32[]{:S(2)}) collective-permute-start(bf16[32,1536]{1,0:T(8,128)(2,1)S(1)} %get-tuple-element.160), channel_id=1, source_target_pairs={{0,12},{4,0},{8,4},{12,8},{1,13},{5,1},{9,5},{13,9},{2,14},{6,2},{... | collective-permute-start | bytes 294920 | tf_op jit(solution)/shard_map/ppermute | solution.py:40
  52.7 10.3 %collective-permute-start.12 = (bf16[32,1536]{1,0:T(8,128)(2,1)S(1)}, bf16[32,1536]{1,0:T(8,128)(2,1)S(1)}, u32[]{:S(2)}, u32[]{:S(2)}) collective-permute-start(bf16[32,1536]{1,0:T(8,128)(2,1)S(1)} %get-tuple-element.161), channel_id=1, source_target_pairs={{0,8},{4,12},{8,0},{12,4},{1,9},{5,13},{9,1},{13,5},{2,10},{6,14},... | collective-permute-start | bytes 294920 | tf_op jit(solution)/shard_map/ppermute | solution.py:40
  53.6 9.4 %collective-permute-start.13 = (bf16[32,1536]{1,0:T(8,128)(2,1)S(1)}, bf16[32,1536]{1,0:T(8,128)(2,1)S(1)}, u32[]{:S(2)}, u32[]{:S(2)}) collective-permute-start(bf16[32,1536]{1,0:T(8,128)(2,1)S(1)} %get-tuple-element.162), channel_id=1, source_target_pairs={{0,4},{4,8},{8,12},{12,0},{1,5},{5,9},{9,13},{13,1},{2,6},{6,10},{... | collective-permute-start | bytes 294920 | tf_op jit(solution)/shard_map/ppermute | solution.py:40

commit v5 on v4

--- a/solution.py
+++ b/solution.py
@@ -282,7 +282,7 @@
     for p, pieces in enumerate(where):
         done = 0
         for three, piece in zip(weights[p], pieces):
-            tile = tile_of(piece[-1])
+            tile = tile_of(piece[-1]) if grads else piece[-1]
             for at in range(0, piece[-1], tile):
                 tiles.append((p, slice(done + at, done + at + tile), three, piece, at))
             done += piece[-1]

time: 63.8 us -> 63.8 us (level)
  transfers between devices with their start and end apart: 14 -> 14, of which waited for: 3 -> 3; matrix products, arithmetic and copies ran while one was open for 0% -> 0% of each run, Pallas kernels for 59% -> 60%
where the time goes in v5:
time: 63.8 us; the launch traced here: 63.7 us
  Pallas kernels  44.7 us (70%)
  starting transfers between devices  15.1 us (24%)
  waiting for transfers between devices  3.05 us (5%)
  between operations  0.82 us (1%)
    pallas_call x5, Pallas kernels, backward(): pl.pallas_call(functools.partial(backward_kernel, where, rows, of or rang...  25.1 us
    ppermute x14, starting transfers between devices, shift(): return lax.ppermute(x, axis, [(i, (i + by) % size) for i in range(size)])  15.1 us
    pallas_call x4, Pallas kernels, forward(): pl.pallas_call(functools.partial(forward_kernel, rows, pieces, ahead, out...  10.8 us
    pallas_call x1, Pallas kernels, load(): pl.pallas_call(functools.partial(load_kernel, pieces), in_specs=[SMEM_SPE...  6.62 us
    ppermute x14, waiting for transfers between devices, shift(): return lax.ppermute(x, axis, [(i, (i + by) % size) for i in range(size)])  3.05 us
  transfers between devices with their start and end apart: 14, of which 3 were waited for; matrix products, arithmetic and copies ran while one was open for 0% of the time, Pallas kernels for 60%

profile of v5, /device:TPU:0, one launch (start us, length us, event | category | flops | bytes accessed | tf_op | source)
XLA Modules:
  0.0 63.7 jit_solution(5523088620852047761)
XLA Ops:
  0.6 0.8 %pack_rows.1.refs_0_ = bf16[32,1536]{1,0:T(8,128)(2,1)S(1)} custom-call(bf16[16,1536]{1,0:T(8,128)(2,1)} %tokens.1, bf16[16,1536]{1,0:T(8,128)(2,1)} %cot.1), custom_call_target="tpu_custom_call" | custom-call | bytes 196608 | tf_op jit(solution)/shard_map/pack_rows/pallas_call | solution.py:116
  1.5 5.1 %collective-permute-start.2 = (bf16[32,1536]{1,0:T(8,128)(2,1)S(1)}, bf16[32,1536]{1,0:T(8,128)(2,1)S(1)}, u32[]{:S(2)}, u32[]{:S(2)}) collective-permute-start(bf16[32,1536]{1,0:T(8,128)(2,1)S(1)} %pack_rows.1.refs_0_), channel_id=1, source_target_pairs={{0,12},{4,0},{8,4},{12,8},{1,13},{5,1},{9,5},{13,9},{2,14},{6,2},{... | collective-permute-start | bytes 294920 | tf_op jit(solution)/shard_map/ppermute | solution.py:40
  6.6 0.0 collective-permute-start.1
  6.6 1.0 %collective-permute-start = (bf16[32,1536]{1,0:T(8,128)(2,1)S(1)}, bf16[32,1536]{1,0:T(8,128)(2,1)S(1)}, u32[]{:S(2)}, u32[]{:S(2)}) collective-permute-start(bf16[32,1536]{1,0:T(8,128)(2,1)S(1)} %pack_rows.1.refs_0_), channel_id=1, source_target_pairs={{0,4},{4,8},{8,12},{12,0},{1,5},{5,9},{9,13},{13,1},{2,6},{6,10},{... | collective-permute-start | bytes 294920 | tf_op jit(solution)/shard_map/ppermute | solution.py:40
  7.6 6.6 %load_weights.1 = (bf16[1536,512]{1,0:T(8,128)(2,1)S(1)}, bf16[1536,512]{1,0:T(8,128)(2,1)S(1)}, bf16[512,1536]{1,0:T(8,128)(2,1)S(1)}, bf16[1536,512]{1,0:T(8,1...) custom-call(s32[1]{0:T(128)} %bitcast.me, ...), custom_call_target="tpu_custom_call" | custom-call | bytes 18874368 | tf_op jit(solution)/shard_map/load_weights/pallas_call | solution.py:90
  14.2 0.0 collective-permute-done.2.refs_3_
  14.2 1.1 %collective-permute-done.1.refs_2_ = bf16[32,1536]{1,0:T(8,128)(2,1)S(1)} collective-permute-done((bf16[32,1536]{1,0:T(8,128)(2,1)S(1)}, bf16[32,1536]{1,0:T(8,128)(2,1)S(1)}, u32[]{:S(2)}, u32[]{:S(2)}) %collective-permute-start.1) | collective-permute-done | bytes 98336 | tf_op jit(solution)/shard_map/ppermute | solution.py:40
  15.3 0.0 collective-permute-done.refs_1_
  15.3 2.4 %partial_sums.4 = (bf16[3,64,1024]{2,1,0:T(8,128)(2,1)S(1)}, bf16[64,1536]{1,0:T(8,128)(2,1)S(1)}, bf16[64,1536]{1,0:T(8,128)(2,1)S(1)}, bf16[1536,512]{1,0:T(8,...) custom-call(s32[1]{0:T(128)} %bitcast.me, bf16[32,1536]{1,0:T(8,128)(2,1)S(1)} %pack_rows.1.refs_0_, ...), custom_call_target="tpu_custom_call" | custom-call | flops 393216 | bytes 393216 | tf_op jit(solution)/shard_map/partial_sums/pallas_call | solution.py:177
  17.7 0.1 collective-permute-start.3
  17.8 2.4 %partial_sums.5 = (f32[3,64,1024]{2,1,0:T(8,128)S(1)}, bf16[1536,512]{1,0:T(8,128)(2,1)S(1)}, bf16[1536,512]{1,0:T(8,128)(2,1)S(1)}, bf16[512,1536]{1,0:T(8,128)(2,1)S(1)}) custom-call(s32[1]{0:T(128)} %bitcast.me, bf16[64,1536]{1,0:T(8,128)(2,1)S(1)} %get-tuple-element.142.refs_0_.refs_8_.refs_2_, ...), custom_call_target="tpu_custom_call" | custom-call | flops 393216 | bytes 393216 | tf_op jit(solution)/shard_map/partial_sums/pallas_call | solution.py:177
  20.3 0.0 collective-permute-done.3.received
  20.3 0.1 join_cores.2
  20.4 1.6 %collective-permute-start.7 = (bf16[3,64,512]{2,1,0:T(8,128)(2,1)S(1)}, bf16[3,64,512]{2,1,0:T(8,128)(2,1)S(1)}, u32[]{:S(2)}, u32[]{:S(2)}) collective-permute-start(bf16[3,64,512]{2,1,0:T(8,128)(2,1)S(1)} %get-tuple-element.140), channel_id=1, source_target_pairs={{0,2},{2,0},{1,3},{3,1},{4,6},{6,4},{5,7},{7,5},{8,10},{10,8},{9,1... | collective-permute-start | bytes 589832 | tf_op jit(solution)/shard_map/ppermute | solution.py:40
  21.9 3.8 %partial_sums.6 = (bf16[3,64,1024]{2,1,0:T(8,128)(2,1)S(1)}, bf16[1536,512]{1,0:T(8,128)(2,1)S(1)}, bf16[1536,512]{1,0:T(8,128)(2,1)S(1)}, bf16[512,1536]{1,0:T(...) custom-call(s32[1]{0:T(128)} %bitcast.me, ...), custom_call_target="tpu_custom_call" | custom-call | flops 393216 | bytes 393216 | tf_op jit(solution)/shard_map/partial_sums/pallas_call | solution.py:177
  25.8 0.3 collective-permute-start.4
  26.1 2.1 %partial_sums.7.mine = f32[3,64,1024]{2,1,0:T(8,128)S(1)} custom-call(s32[1]{0:T(128)} %bitcast.me, bf16[64,1536]{1,0:T(8,128)(2,1)S(1)} %get-tuple-element.142.refs_0_.refs_8_.refs_2_, bf16[64,1536]{1,0:T(8,128)(2,1)S(1)} %get-tuple-element.143.refs_1_.refs_9_.refs_3_, bf16[1536,512]{1,0:T(8,128)(2,1)S(1)} %get-tuple-element.129.refs_2_.refs_1_, ...), custom_call_target="tpu_custom_call" | custom-call | flops 393216 | bytes 393216 | tf_op jit(solution)/shard_map/partial_sums/pallas_call | solution.py:177
  28.2 0.0 collective-permute-done.7.refs_1_
  28.2 0.1 activation.3.refs_0_
  28.3 0.4 collective-permute-start.8
  28.7 0.8 %collective-permute-start.6 = (bf16[3,64,512]{2,1,0:T(8,128)(2,1)S(1)}, bf16[3,64,512]{2,1,0:T(8,128)(2,1)S(1)}, u32[]{:S(2)}, u32[]{:S(2)}) collective-permute-start(bf16[3,64,512]{2,1,0:T(8,128)(2,1)S(1)} %get-tuple-element.120), channel_id=1, source_target_pairs={{0,2},{2,0},{1,3},{3,1},{4,6},{6,4},{5,7},{7,5},{8,10},{10,8},{9,1... | collective-permute-start | bytes 589832 | tf_op jit(solution)/shard_map/ppermute | solution.py:40
  29.5 0.0 collective-permute-done.4.received
  29.5 0.1 join_cores.3
  29.6 1.3 %collective-permute-start.5 = (bf16[3,64,1024]{2,1,0:T(8,128)(2,1)S(1)}, bf16[3,64,1024]{2,1,0:T(8,128)(2,1)S(1)}, u32[]{:S(2)}, u32[]{:S(2)}) collective-permute-start(bf16[3,64,1024]{2,1,0:T(8,128)(2,1)S(1)} %get-tuple-element.137), channel_id=1, source_target_pairs={{0,2},{2,0},{1,3},{3,1},{4,6},{6,4},{5,7},{7,5},{8,10},{10,8},{9,1... | collective-permute-start | bytes 1179656 | tf_op jit(solution)/shard_map/ppermute | solution.py:40
  30.9 0.0 collective-permute-done.8.refs_1_
  30.9 6.2 %backward.2 = (f32[64,1536]{1,0:T(8,128)S(1)}, f32[64,1536]{1,0:T(8,128)S(1)}, bf16[1536,4096]{1,0:T(8,128)(2,1)}, bf16[1536,4096]{1,0:T(8,128)(2,1)}, bf16[4096,1536]{1,0:T(8,128)(2,1)}) custom-call(s32[1]{0:T(128)} %bitcast.me, bf16[3,64,512]{2,1,0:T(8,128)(2,1)S(1)} %activation.3.refs_0_, bf16[3,64,512]{2,1,0:T(8,128)(2,1)S(1)} %collective-permute-done.8.refs_1_, ...), custom_call_target="tpu_custom_call" | custom-call | flops 1207959552 | bytes 18874368 | tf_op jit(solution)/shard_map/backward/pallas_call | solution.py:370
  37.1 0.0 collective-permute-done.6.refs_1_
  37.1 0.1 activation.4.refs_0_
  37.2 0.1 collective-permute-start.9
  37.3 1.4 %collective-permute-done.9.refs_1_ = bf16[3,64,512]{2,1,0:T(8,128)(2,1)S(1)} collective-permute-done((bf16[3,64,512]{2,1,0:T(8,128)(2,1)S(1)}, bf16[3,64,512]{2,1,0:T(8,128)(2,1)S(1)}, u32[]{:S(2)}, u32[]{:S(2)}) %collective-permute-start.9) | collective-permute-done | bytes 196640 | tf_op jit(solution)/shard_map/ppermute | solution.py:40
  38.7 6.5 %backward.3 = (f32[64,1536]{1,0:T(8,128)S(1)}, f32[64,1536]{1,0:T(8,128)S(1)}, bf16[1536,4096]{1,0:T(8,128)(2,1)}, bf16[1536,4096]{1,0:T(8,128)(2,1)}, bf16[4096,1536]{1,0:T(8,128)(2,1)}) custom-call(s32[1]{0:T(128)} %bitcast.me, bf16[3,64,512]{2,1,0:T(8,128)(2,1)S(1)} %activation.4.refs_0_, ...), custom_call_target="tpu_custom_call", output_to_operand_aliasing={{2}: (13, {}), {3}: (14, {}), {4}: (15, {})} | custom-call | flops 1207959552 | bytes 18874368 | tf_op jit(solution)/shard_map/backward/pallas_call | solution.py:370
  45.2 0.0 collective-permute-done.5.refs_1_
  45.2 0.2 activation.5.refs_0_
  45.4 0.2 collective-permute-start.10
  45.6 2.6 %output_rows.2 = (f32[64,1536]{1,0:T(8,128)S(1)}, f32[64,1536]{1,0:T(8,128)S(1)}) custom-call(s32[1]{0:T(128)} %bitcast.me, bf16[3,64,1024]{2,1,0:T(8,128)(2,1)S(1)} %activation.5.refs_0_, bf16[1536,512]{1,0:T(8,128)(2,1)S(1)} %get-tuple-element.129.refs_2_.refs_1_, bf16[1536,512]{1,0:T(8,128)(2,1)S(1)} %get-tuple-element.130.refs_3_.refs_2_, ...), custom_call_target="tpu_custom_call" | custom-call | flops 603979776 | bytes 9437184 | tf_op jit(solution)/shard_map/output_rows/pallas_call | solution.py:370
  48.1 0.0 collective-permute-done.10.refs_0_.refs_1_
  48.2 2.5 %output_rows.3 = (f32[32,1536]{1,0:T(8,128)S(1)}, bf16[32,1536]{1,0:T(8,128)(2,1)S(1)}, bf16[32,1536]{1,0:T(8,128)(2,1)S(1)}, bf16[32,1536]{1,0:T(8,128)(2,1)S(1)}) custom-call(s32[1]{0:T(128)} %bitcast.me, bf16[3,64,1024]{2,1,0:T(8,128)(2,1)S(1)} %collective-permute-done.10.refs_0_.refs_1_, bf16[1536,512]{1,0:T(8,128)(2,1)S(1)} %get-tuple-element.123.refs_2_.refs_1_, ...), custom_call_target="tpu_custom_call" | custom-call | flops 603979776 | bytes 9437184 | tf_op jit(solution)/shard_map/output_rows/pallas_call | solution.py:370
  50.7 2.0 %collective-permute-start.11 = (bf16[32,1536]{1,0:T(8,128)(2,1)S(1)}, bf16[32,1536]{1,0:T(8,128)(2,1)S(1)}, u32[]{:S(2)}, u32[]{:S(2)}) collective-permute-start(bf16[32,1536]{1,0:T(8,128)(2,1)S(1)} %get-tuple-element.160), channel_id=1, source_target_pairs={{0,12},{4,0},{8,4},{12,8},{1,13},{5,1},{9,5},{13,9},{2,14},{6,2},{... | collective-permute-start | bytes 294920 | tf_op jit(solution)/shard_map/ppermute | solution.py:40
  52.7 0.9 %collective-permute-start.12 = (bf16[32,1536]{1,0:T(8,128)(2,1)S(1)}, bf16[32,1536]{1,0:T(8,128)(2,1)S(1)}, u32[]{:S(2)}, u32[]{:S(2)}) collective-permute-start(bf16[32,1536]{1,0:T(8,128)(2,1)S(1)} %get-tuple-element.161), channel_id=1, source_target_pairs={{0,8},{4,12},{8,0},{12,4},{1,9},{5,13},{9,1},{13,5},{2,10},{6,14},... | collective-permute-start | bytes 294920 | tf_op jit(solution)/shard_map/ppermute | solution.py:40
  53.6 1.4 %collective-permute-start.13 = (bf16[32,1536]{1,0:T(8,128)(2,1)S(1)}, bf16[32,1536]{1,0:T(8,128)(2,1)S(1)}, u32[]{:S(2)}, u32[]{:S(2)}) collective-permute-start(bf16[32,1536]{1,0:T(8,128)(2,1)S(1)} %get-tuple-element.162), channel_id=1, source_target_pairs={{0,4},{4,8},{8,12},{12,0},{1,5},{5,9},{9,13},{13,1},{2,6},{6,10},{... | collective-permute-start | bytes 294920 | tf_op jit(solution)/shard_map/ppermute | solution.py:40
  55.1 7.4 %weight_grads.1 = (bf16[1536,4096]{1,0:T(8,128)(2,1)}, bf16[1536,4096]{1,0:T(8,128)(2,1)}, bf16[4096,1536]{1,0:T(8,128)(2,1)}) custom-call(s32[1]{0:T(128)} %bitcast.me, bf16[3,64,1024]{2,1,0:T(8,128)(2,1)S(1)} %activation.5.refs_0_, ...), custom_call_target="tpu_custom_call", output_to_operand_aliasing={{0}: (5, {}), {1}: (6, {}), {2}: (7, {})} | custom-call | flops 1207959552 | bytes 18874368 | tf_op jit(solution)/shard_map/weight_grads/pallas_call | solution.py:370
  62.5 0.0 collective-permute-done.11.refs_1_
  62.5 0.5 collective-permute-done.12.refs_2_
  63.0 0.0 collective-permute-done.13.refs_3_
  63.0 0.7 %finish_rows.1 = (bf16[16,1536]{1,0:T(8,128)(2,1)}, bf16[16,1536]{1,0:T(8,128)(2,1)}) custom-call(f32[32,1536]{1,0:T(8,128)S(1)} %get-tuple-element.159.refs_0_, bf16[32,1536]{1,0:T(8,128)(2,1)S(1)} %collective-permute-done.11.refs_1_, bf16[32,1536]{1,0:T(8,128)(2,1)S(1)} %collective-permute-done.12.refs_2_, bf16[32,1536]{1,0:T(8,128)(2,1)S(1)} %collective-permute-done.13.refs_3_), custom_call_target="tpu_custom_call" | custom-call | tf_op jit(solution)/shard_map/finish_rows/pallas_call | solution.py:399
Async XLA Ops:
  1.5 12.8 %collective-permute-start.2 = (bf16[32,1536]{1,0:T(8,128)(2,1)S(1)}, bf16[32,1536]{1,0:T(8,128)(2,1)S(1)}, u32[]{:S(2)}, u32[]{:S(2)}) collective-permute-start(bf16[32,1536]{1,0:T(8,128)(2,1)S(1)} %pack_rows.1.refs_0_), channel_id=1, source_target_pairs={{0,12},{4,0},{8,4},{12,8},{1,13},{5,1},{9,5},{13,9},{2,14},{6,2},{... | collective-permute-start | bytes 294920 | tf_op jit(solution)/shard_map/ppermute | solution.py:40
  6.6 8.7 %collective-permute-start.1 = (bf16[32,1536]{1,0:T(8,128)(2,1)S(1)}, bf16[32,1536]{1,0:T(8,128)(2,1)S(1)}, u32[]{:S(2)}, u32[]{:S(2)}) collective-permute-start(bf16[32,1536]{1,0:T(8,128)(2,1)S(1)} %pack_rows.1.refs_0_), channel_id=1, source_target_pairs={{0,8},{4,12},{8,0},{12,4},{1,9},{5,13},{9,1},{13,5},{2,10},{6,14},... | collective-permute-start | bytes 294920 | tf_op jit(solution)/shard_map/ppermute | solution.py:40
  6.6 8.7 %collective-permute-start = (bf16[32,1536]{1,0:T(8,128)(2,1)S(1)}, bf16[32,1536]{1,0:T(8,128)(2,1)S(1)}, u32[]{:S(2)}, u32[]{:S(2)}) collective-permute-start(bf16[32,1536]{1,0:T(8,128)(2,1)S(1)} %pack_rows.1.refs_0_), channel_id=1, source_target_pairs={{0,4},{4,8},{8,12},{12,0},{1,5},{5,9},{9,13},{13,1},{2,6},{6,10},{... | collective-permute-start | bytes 294920 | tf_op jit(solution)/shard_map/ppermute | solution.py:40
  17.7 2.5 %collective-permute-start.3 = (bf16[3,64,1024]{2,1,0:T(8,128)(2,1)S(1)}, bf16[3,64,1024]{2,1,0:T(8,128)(2,1)S(1)}, u32[]{:S(2)}, u32[]{:S(2)}) collective-permute-start(bf16[3,64,1024]{2,1,0:T(8,128)(2,1)S(1)} %get-tuple-element.119), channel_id=1, source_target_pairs={{0,1},{1,0},{2,3},{3,2},{4,5},{5,4},{6,7},{7,6},{8,9},{9,8},{10,11... | collective-permute-start | bytes 1179656 | tf_op jit(solution)/shard_map/ppermute | solution.py:40
  20.4 7.8 %collective-permute-start.7 = (bf16[3,64,512]{2,1,0:T(8,128)(2,1)S(1)}, bf16[3,64,512]{2,1,0:T(8,128)(2,1)S(1)}, u32[]{:S(2)}, u32[]{:S(2)}) collective-permute-start(bf16[3,64,512]{2,1,0:T(8,128)(2,1)S(1)} %get-tuple-element.140), channel_id=1, source_target_pairs={{0,2},{2,0},{1,3},{3,1},{4,6},{6,4},{5,7},{7,5},{8,10},{10,8},{9,1... | collective-permute-start | bytes 589832 | tf_op jit(solution)/shard_map/ppermute | solution.py:40
  25.8 3.7 %collective-permute-start.4 = (bf16[3,64,1024]{2,1,0:T(8,128)(2,1)S(1)}, bf16[3,64,1024]{2,1,0:T(8,128)(2,1)S(1)}, u32[]{:S(2)}, u32[]{:S(2)}) collective-permute-start(bf16[3,64,1024]{2,1,0:T(8,128)(2,1)S(1)} %get-tuple-element.135), channel_id=1, source_target_pairs={{0,1},{1,0},{2,3},{3,2},{4,5},{5,4},{6,7},{7,6},{8,9},{9,8},{10,11... | collective-permute-start | bytes 1179656 | tf_op jit(solution)/shard_map/ppermute | solution.py:40
  28.3 2.6 %collective-permute-start.8 = (bf16[3,64,512]{2,1,0:T(8,128)(2,1)S(1)}, bf16[3,64,512]{2,1,0:T(8,128)(2,1)S(1)}, u32[]{:S(2)}, u32[]{:S(2)}) collective-permute-start(bf16[3,64,512]{2,1,0:T(8,128)(2,1)S(1)} %activation.3.refs_0_), channel_id=1, source_target_pairs={{0,1},{1,0},{2,3},{3,2},{4,5},{5,4},{6,7},{7,6},{8,9},{9,8},{10,11... | collective-permute-start | bytes 589832 | tf_op jit(solution)/shard_map/ppermute | solution.py:40
  28.7 8.4 %collective-permute-start.6 = (bf16[3,64,512]{2,1,0:T(8,128)(2,1)S(1)}, bf16[3,64,512]{2,1,0:T(8,128)(2,1)S(1)}, u32[]{:S(2)}, u32[]{:S(2)}) collective-permute-start(bf16[3,64,512]{2,1,0:T(8,128)(2,1)S(1)} %get-tuple-element.120), channel_id=1, source_target_pairs={{0,2},{2,0},{1,3},{3,1},{4,6},{6,4},{5,7},{7,5},{8,10},{10,8},{9,1... | collective-permute-start | bytes 589832 | tf_op jit(solution)/shard_map/ppermute | solution.py:40
  29.6 15.6 %collective-permute-start.5 = (bf16[3,64,1024]{2,1,0:T(8,128)(2,1)S(1)}, bf16[3,64,1024]{2,1,0:T(8,128)(2,1)S(1)}, u32[]{:S(2)}, u32[]{:S(2)}) collective-permute-start(bf16[3,64,1024]{2,1,0:T(8,128)(2,1)S(1)} %get-tuple-element.137), channel_id=1, source_target_pairs={{0,2},{2,0},{1,3},{3,1},{4,6},{6,4},{5,7},{7,5},{8,10},{10,8},{9,1... | collective-permute-start | bytes 1179656 | tf_op jit(solution)/shard_map/ppermute | solution.py:40
  37.2 1.5 %collective-permute-start.9 = (bf16[3,64,512]{2,1,0:T(8,128)(2,1)S(1)}, bf16[3,64,512]{2,1,0:T(8,128)(2,1)S(1)}, u32[]{:S(2)}, u32[]{:S(2)}) collective-permute-start(bf16[3,64,512]{2,1,0:T(8,128)(2,1)S(1)} %activation.4.refs_0_), channel_id=1, source_target_pairs={{0,1},{1,0},{2,3},{3,2},{4,5},{5,4},{6,7},{7,6},{8,9},{9,8},{10,11... | collective-permute-start | bytes 589832 | tf_op jit(solution)/shard_map/ppermute | solution.py:40
  45.4 2.8 %collective-permute-start.10 = (bf16[3,64,1024]{2,1,0:T(8,128)(2,1)S(1)}, bf16[3,64,1024]{2,1,0:T(8,128)(2,1)S(1)}, u32[]{:S(2)}, u32[]{:S(2)}) collective-permute-start(bf16[3,64,1024]{2,1,0:T(8,128)(2,1)S(1)} %activation.5.refs_0_), channel_id=1, source_target_pairs={{0,1},{1,0},{2,3},{3,2},{4,5},{5,4},{6,7},{7,6},{8,9},{9,8},{10,11... | collective-permute-start | bytes 1179656 | tf_op jit(solution)/shard_map/ppermute | solution.py:40
  50.7 11.8 %collective-permute-start.11 = (bf16[32,1536]{1,0:T(8,128)(2,1)S(1)}, bf16[32,1536]{1,0:T(8,128)(2,1)S(1)}, u32[]{:S(2)}, u32[]{:S(2)}) collective-permute-start(bf16[32,1536]{1,0:T(8,128)(2,1)S(1)} %get-tuple-element.160), channel_id=1, source_target_pairs={{0,12},{4,0},{8,4},{12,8},{1,13},{5,1},{9,5},{13,9},{2,14},{6,2},{... | collective-permute-start | bytes 294920 | tf_op jit(solution)/shard_map/ppermute | solution.py:40
  52.7 10.3 %collective-permute-start.12 = (bf16[32,1536]{1,0:T(8,128)(2,1)S(1)}, bf16[32,1536]{1,0:T(8,128)(2,1)S(1)}, u32[]{:S(2)}, u32[]{:S(2)}) collective-permute-start(bf16[32,1536]{1,0:T(8,128)(2,1)S(1)} %get-tuple-element.161), channel_id=1, source_target_pairs={{0,8},{4,12},{8,0},{12,4},{1,9},{5,13},{9,1},{13,5},{2,10},{6,14},... | collective-permute-start | bytes 294920 | tf_op jit(solution)/shard_map/ppermute | solution.py:40
  53.6 9.4 %collective-permute-start.13 = (bf16[32,1536]{1,0:T(8,128)(2,1)S(1)}, bf16[32,1536]{1,0:T(8,128)(2,1)S(1)}, u32[]{:S(2)}, u32[]{:S(2)}) collective-permute-start(bf16[32,1536]{1,0:T(8,128)(2,1)S(1)} %get-tuple-element.162), channel_id=1, source_target_pairs={{0,4},{4,8},{8,12},{12,0},{1,5},{5,9},{9,13},{13,1},{2,6},{6,10},{... | collective-permute-start | bytes 294920 | tf_op jit(solution)/shard_map/ppermute | solution.py:40
